TPU v7x, 32 devices: a whole 2x2x4 slice. The times are simulated.
32 devices in a mesh: groups: 2 (over x), dom: 16 (over z, y, core).
Axes of the slice: x: 2, y: 2, z: 4, core: 2. Of those that a mesh axis runs over, the one named last changes fastest.
Arguments:
- grid: bfloat16 [32768, 1024], P(('groups', 'dom')), parts along dimension 0, may hold values from -6 to 6
- latent_in: bfloat16 [512, 1024], P(('groups', 'dom')), parts along dimension 0, may hold values from -3 to 3
- grid_gain: float32 [1024], replicated, may hold values from 0.5 to 1.5
- node_gain: float32 [1024], replicated, may hold values from 0.5 to 1.5
- dec_gain: float32 [1024], replicated, may hold values from 0.5 to 1.5
- w_q_enc: bfloat16 [1024, 512], replicated
- w_kv_enc: bfloat16 [1024, 1024], replicated, may hold values from -0.1875 to 0.1875
- w_o_enc: bfloat16 [512, 1024], replicated, may hold values from -0.25 to 0.25
- w_q_dec: bfloat16 [1024, 512], replicated
- w_kv_dec: bfloat16 [1024, 1024], replicated, may hold values from -0.1875 to 0.1875
- w_o_dec: bfloat16 [512, 1024], replicated, may hold values from -0.25 to 0.25
- enc_need: int32 [16, 512], P('dom'), may hold values from 0 to 1023
- enc_slot: int32 [32, 256], P(None, 'dom'), may hold values from 0 to 511
- enc_count: int32 [256], P('dom'), may hold values from 1 to 32
- dec_need: int32 [16, 4096], P('dom'), may hold values from 0 to 15
- dec_slot: int32 [4, 16384], P(None, 'dom'), may hold values from 0 to 4095
Outputs:
- latent_out: bfloat16 [512, 1024], P(('groups', 'dom')), parts along dimension 0
- grid_out: bfloat16 [32768, 1024], P(('groups', 'dom')), parts along dimension 0
There are 2 independent parts, one for each index of `groups`. A program takes and returns all parts, laid end to end along the dimension named above; an argument that names none is the same for every part. Nothing has to cross between parts.
Inputs may be any that keep to these rules, and one draw needn't show every extreme that they name: `enc_need`: a grid point's index within its band; entries may repeat. Edges of node n are enc_slot[0..enc_count[n]-1, n]; entries may repeat. `dec_need`: a latent node's index within its window; entries may repeat. `dec_slot`: entries may repeat.
All inputs are finite; a program needn't handle non-finite values.
Results may differ from a plain program's by a relative error of at most 0.02.
The roundings to bfloat16 on the way count: a program that leaves them out, or rounds other values in their place, can miss the bound.
Values may be sent and summed in bfloat16 or wider, within the bound.
A program may use at most 128 MiB of HBM per device.

v0:
```python
import math

import jax
import jax.numpy as jnp
from jax import lax
from jax.sharding import PartitionSpec as P

HEADS = 8


norm_eps = 1e-06


def rms_norm(values, weight_gain):
    widened = values.astype(jnp.float32)
    spread = jnp.mean(widened * widened, axis=-1, keepdims=True)
    return (widened * lax.rsqrt(spread + norm_eps) * weight_gain).astype(jnp.bfloat16)


def attend_keys(queries, key_rows, keep_mask):
    rows_here = queries.shape[0]
    inner_width = queries.shape[1]
    head_size = inner_width // HEADS
    edge_count = key_rows.shape[0]
    query_heads = queries.reshape(rows_here, HEADS, head_size)
    key_heads = key_rows[..., :inner_width].reshape(edge_count, rows_here, HEADS, head_size)
    value_heads = key_rows[..., inner_width:].reshape(edge_count, rows_here, HEADS, head_size)
    scores = jnp.einsum(
        "rhd,krhd->krh", query_heads, key_heads, preferred_element_type=jnp.float32
    ) * (1.0 / math.sqrt(head_size))
    if keep_mask is not None:
        scores = jnp.where(keep_mask[:, :, None], scores, -1e30)
    highest = jnp.max(scores, axis=0, keepdims=True)
    raised = jnp.exp(scores - highest)
    weights = (raised / jnp.sum(raised, axis=0, keepdims=True)).astype(jnp.bfloat16)
    mixed = jnp.einsum("krh,krhd->rhd", weights, value_heads, preferred_element_type=jnp.float32)
    return mixed.reshape(rows_here, inner_width).astype(jnp.bfloat16)


def on_device(
    grid,
    latent_in,
    grid_gain,
    node_gain,
    dec_gain,
    w_q_enc,
    w_kv_enc,
    w_o_enc,
    w_q_dec,
    w_kv_dec,
    w_o_dec,
    enc_need,
    enc_slot,
    enc_count,
    dec_need,
    dec_slot,
):
    peer_count = lax.axis_size("dom")
    normed_grid = rms_norm(grid, grid_gain)
    requests = enc_need.reshape(peer_count, -1)
    wanted = lax.all_to_all(requests, "dom", split_axis=0, concat_axis=0, tiled=True)
    source_rows = jnp.dot(normed_grid, w_kv_enc, preferred_element_type=jnp.float32).astype(
        jnp.bfloat16
    )
    arrived = lax.all_to_all(source_rows[wanted], "dom", split_axis=0, concat_axis=0, tiled=True)
    arrived = arrived.reshape(-1, arrived.shape[-1])
    enc_queries = jnp.dot(
        rms_norm(latent_in, node_gain), w_q_enc, preferred_element_type=jnp.float32
    ).astype(jnp.bfloat16)
    keep_mask = jnp.arange(enc_slot.shape[0], dtype=jnp.int32)[:, None] < enc_count[None, :]
    enc_mixed = attend_keys(enc_queries, arrived[enc_slot], keep_mask)
    enc_update = jnp.dot(enc_mixed, w_o_enc, preferred_element_type=jnp.float32)
    latent_out = (latent_in.astype(jnp.float32) + enc_update).astype(jnp.bfloat16)
    latent_pairs = jnp.dot(
        rms_norm(latent_out, dec_gain), w_kv_dec, preferred_element_type=jnp.float32
    ).astype(jnp.bfloat16)
    dec_queries = jnp.dot(normed_grid, w_q_dec, preferred_element_type=jnp.float32).astype(
        jnp.bfloat16
    )
    everyone = lax.all_gather(latent_pairs, "dom", axis=0, tiled=True)
    slot_total = dec_need.shape[1]
    dec_cap = slot_total // peer_count
    owner_rows = jnp.arange(slot_total, dtype=jnp.int32) // dec_cap
    global_rows = owner_rows * latent_pairs.shape[0] + dec_need[0]
    dec_keys = everyone[global_rows[dec_slot]]
    dec_mixed = attend_keys(dec_queries, dec_keys, None)
    dec_update = jnp.dot(dec_mixed, w_o_dec, preferred_element_type=jnp.float32)
    grid_out = (grid.astype(jnp.float32) + dec_update).astype(jnp.bfloat16)
    return (latent_out, grid_out)


def solution(mesh):
    return jax.shard_map(
        on_device,
        mesh=mesh,
        in_specs=(
            P(("groups", "dom"), None),
            P(("groups", "dom"), None),
            P(),
            P(),
            P(),
            P(),
            P(),
            P(),
            P(),
            P(),
            P(),
            P("dom", None),
            P(None, "dom"),
            P("dom"),
            P("dom", None),
            P(None, "dom"),
        ),
        out_specs=(P(("groups", "dom"), None), P(("groups", "dom"), None)),
        check_vma=False,
    )
```

profile of v0, /device:TPU:0, one launch (start us, length us, event | category | flops | bytes accessed | tf_op | source)
XLA Modules:
  0.0 145.5 jit_solution(9233177008498145265)
XLA Ops:
  0.6 0.0 copy-start
  0.6 0.5 broadcast.131
  1.2 1.5 reduce.7
  2.6 0.7 all_to_all.11
  3.3 7.4 %all-to-all-start = ((s32[16,1,32]{2,1,0:T(1,128)}), s32[16,1,32]{2,1,0:T(1,128)S(1)}, u32[]{:S(2)}, u32[]{:S(2)}) async-start(s32[16,1,32]{2,1,0:T(1,128)} %all_to_all.11), calls=%async_computation | async-start | bytes 16384 | tf_op jit(solution)/shard_map/all_to_all | solution.py:61
  10.7 2.1 %fusion.2 = f32[1024]{0:T(1024)S(1)} fusion(bf16[1024,1024]{1,0:T(8,128)(2,1)} %param.16), kind=kLoop, calls=%fused_computation.11 | loop fusion | flops 3144704 | bytes 2101248 | tf_op jit(solution)/shard_map/reduce_sum | solution.py:16
  12.8 0.7 compare_select_fusion.2
  13.5 0.0 copy-done
  13.5 0.0 copy-start.2
  13.5 5.3 %convolution_convert_fusion = bf16[1024,1024]{1,0:T(8,128)(2,1)} fusion(bf16[1024,1024]{1,0:T(8,128)(2,1)S(1)} %copy-done, bf16[1024,1024]{1,0:T(8,128)(2,1)} %param.16, f32[1024]{0:T(1024)} %param.18, f32[1024]{0:T(1024)S(1)} %add_rsqrt_fusion), kind=kOutput, calls=%fused_computation.15 | convolution fusion | flops 2152726528 | bytes 6299648 | tf_op jit(solution)/shard_map/dot_general | solution.py:62
  18.8 0.0 copy-done.2
  18.8 0.1 fusion.23
  18.9 0.0 all-to-all-done
  19.0 0.1 reshape.132
  19.0 0.0 copy-start.6
  19.0 0.0 copy-start.4
  19.1 0.0 copy-start.5
  19.1 5.4 %gather_fusion = bf16[512,1024]{1,0:T(8,128)(2,1)} fusion(bf16[1024,1024]{1,0:T(8,128)(2,1)} %convolution_convert_fusion, s32[1024]{0:T(1024)S(1)} %pad_clamp_fusion.1), kind=kCustom, calls=%fused_computation | custom fusion | bytes 2099200 | tf_op jit(solution)/shard_map/gather | solution.py:65
  24.4 6.0 %all-to-all-start.1 = ((bf16[16,32,1024]{2,1,0:T(8,128)(2,1)}), bf16[16,32,1024]{2,1,0:T(8,128)(2,1)S(1)}, u32[]{:S(2)}, u32[]{:S(2)}) async-start(bf16[16,32,1024]{2,1,0:T(8,128)(2,1)} %bitcast.66), calls=%async_computation.1 | async-start | bytes 2097152 | tf_op jit(solution)/shard_map/all_to_all | solution.py:65
  30.5 0.1 copy.24
  30.5 0.1 reshape.140
  30.6 0.0 copy-done.6
  30.6 1.5 %convolution_convert_fusion.3 = bf16[16,512]{1,0:T(8,128)(2,1)S(1)} fusion(bf16[1024,512]{1,0:T(8,128)(2,1)} %param.21, bf16[16,1024]{1,0:T(8,128)(2,1)S(1)} %copy-done.2, f32[1024]{0:T(1024)S(1)} %copy-done.6, f32[16]{0:T(128)S(1)} %add_rsqrt_fusion.2), kind=kOutput, calls=%fused_computation.25 | convolution fusion | flops 16850944 | bytes 1101888 | tf_op jit(solution)/shard_map/dot_general | solution.py:67
  32.1 0.1 reshape.178
  32.2 0.0 copy-done.4
  32.3 0.0 copy-done.5
  32.3 0.0 copy-start.8
  32.3 0.0 copy-start.10
  32.3 23.0 %gather_fusion.2 = s32[4096]{0:T(1024)S(1)} fusion(s32[4096]{0:T(1024)S(1)} %get-tuple-element.8, s32[4096]{0:T(1024)S(1)} %get-tuple-element.9), kind=kCustom, calls=%fused_computation.2 | custom fusion | bytes 49152 | tf_op jit(solution)/shard_map/gather | solution.py:85
  55.4 0.0 copy-done.8
  55.4 0.1 iota_compare_fusion
  55.5 0.0 copy-done.10
  55.5 4.6 %bitcast_convert_fusion.1 = f32[1024,8,64]{0,2,1:T(8,128)} fusion(bf16[1024,512]{1,0:T(8,128)(2,1)} %param.24, bf16[1024,1024]{1,0:T(8,128)(2,1)} %param.16, f32[1024]{0:T(1024)S(1)} %copy-done.10, f32[1024]{0:T(1024)S(1)} %add_rsqrt_fusion), kind=kOutput, calls=%fused_computation.79 | convolution fusion | flops 1078984704 | bytes 5251072 | tf_op jit(solution)/shard_map/dot_general | solution.py:77
  60.1 0.0 all-to-all-done.1
  60.1 2.8 %gather_fusion.1 = bf16[512,1024]{1,0:T(8,128)(2,1)} fusion(bf16[512,1024]{1,0:T(8,128)(2,1)S(1)} %bitcast.62, s32[1024]{0:T(1024)S(1)} %pad_clamp_fusion), kind=kCustom, calls=%fused_computation.1 | custom fusion | bytes 2099200 | tf_op jit(solution)/shard_map/gather | solution.py:71
  62.9 1.3 fusion.47
  64.2 0.0 copy-start.7
  64.2 1.6 %reshape.124 = bf16[32,16,8,64]{3,2,1,0:T(8,128)(2,1)} reshape(bf16[32,16,512]{2,1,0:T(8,128)(2,1)S(1)} %get-tuple-element.4) | data formatting | bytes 1048576 | tf_op jit(solution)/shard_map/reshape | solution.py:26
  65.8 1.5 %reshape.126 = bf16[32,16,8,64]{3,2,1,0:T(8,128)(2,1)} reshape(bf16[32,16,512]{2,1,0:T(8,128)(2,1)S(1)} %get-tuple-element.5) | data formatting | bytes 1048576 | tf_op jit(solution)/shard_map/reshape | solution.py:27
  67.3 2.0 %fusion.14 = f32[16,8,1,32]{3,2,1,0:T(1,128)S(1)} fusion(bf16[16,8,64,1]{2,3,1,0:T(2,128)(2,1)S(1)} %reshape.178, bf16[32,16,8,64]{3,2,1,0:T(8,128)(2,1)} %reshape.124), kind=kOutput, calls=%fused_computation.28 | convolution fusion | flops 524288 | bytes 557056 | tf_op jit(solution)/shard_map/rhd,krhd->krh/dot_general | solution.py:28
  69.2 0.2 fusion.11
  69.4 1.9 %fusion.12 = f32[16,8,1,64]{3,2,1,0:T(1,128)S(1)} fusion(bf16[32,16,8,64]{3,2,1,0:T(8,128)(2,1)} %reshape.126, bf16[32,16,8,1]{0,2,1,3:T(8,128)(2,1)S(1)} %fusion.11), kind=kOutput, calls=%fused_computation.26 | convolution fusion | flops 524288 | bytes 565248 | tf_op jit(solution)/shard_map/krh,krhd->rhd/dot_general | solution.py:36
  71.4 0.1 convert_element_type.64
  71.5 1.6 %fusion.20 = (f32[16]{0:T(128)S(1)}, bf16[16,1024]{1,0:T(8,128)(2,1)S(1)}) fusion(bf16[16,512]{1,0:T(8,128)(2,1)S(1)} %convert_element_type.64, bf16[512,1024]{1,0:T(8,128)(2,1)} %param.23, bf16[16,1024]{1,0:T(8,128)(2,1)S(1)} %copy-done.2), kind=kOutput, calls=%fused_computation.39 | convolution fusion | flops 16875504 | bytes 1130560 | tf_op jit(solution)/shard_map/dot_general | solution.py:72
  73.1 0.0 copy-start.3
  73.1 0.0 copy-done.7
  73.1 2.0 %convolution_convert_fusion.2 = bf16[16,1024]{1,0:T(8,128)(2,1)S(1)} fusion(bf16[1024,1024]{1,0:T(8,128)(2,1)} %param.25, bf16[16,1024]{1,0:T(8,128)(2,1)S(1)} %get-tuple-element.7, f32[1024]{0:T(1024)S(1)} %copy-done.7, f32[16]{0:T(128)S(1)} %add_rsqrt_fusion.1), kind=kOutput, calls=%fused_computation.23 | convolution fusion | flops 33636352 | bytes 2166848 | tf_op jit(solution)/shard_map/dot_general | solution.py:74
  75.1 23.4 %all_gather.3 = bf16[256,1024]{1,0:T(8,128)(2,1)S(1)} all-gather(bf16[16,1024]{1,0:T(8,128)(2,1)S(1)} %convolution_convert_fusion.2), channel_id=1, replica_groups=mesh['groups'=2,'dom'=16] {'dom'}, dimensions={0}, use_global_device_ids=true | all-gather | bytes 557056 | tf_op jit(solution)/shard_map/all_gather | solution.py:80
  98.6 18.3 %gather_fusion.3 = bf16[4096,1024]{1,0:T(8,128)(2,1)} fusion(bf16[256,1024]{1,0:T(8,128)(2,1)S(1)} %all_gather.3, s32[4096]{0:T(1024)S(1)} %bitcast_clamp_fusion), kind=kCustom, calls=%fused_computation.3 | custom fusion | bytes 16793600 | tf_op jit(solution)/shard_map/gather | solution.py:85
  116.8 0.0 copy-done.3
  116.8 5.7 %fusion.46 = (bf16[4,1024,512]{2,1,0:T(8,128)(2,1)}, bf16[4,1024,512]{2,1,0:T(8,128)(2,1)}) fusion(bf16[4,1024,1024]{2,1,0:T(8,128)(2,1)} %bitcast.63), kind=kLoop, calls=%fused_computation.82 | loop fusion | bytes 16777216 | tf_op jit(solution)/shard_map/slice | solution.py:26
  122.6 6.3 %copy.45 = bf16[4,1024,512]{1,2,0:T(8,128)(2,1)} copy(bf16[4,1024,512]{2,1,0:T(8,128)(2,1)} %get-tuple-element.2) | data formatting | bytes 8388608
  128.9 4.1 %multiply_reduce_fusion.1 = f32[1024,8,4]{0,1,2:T(8,128)S(1)} fusion(f32[1024,8,64]{0,2,1:T(8,128)} %bitcast_convert_fusion.1, bf16[4,1024,512]{1,2,0:T(8,128)(2,1)} %copy.45), kind=kLoop, calls=%fused_computation.7 | loop fusion | flops 6258688 | bytes 6422528 | tf_op jit(solution)/shard_map/rhd,krhd->krh/dot_general | solution.py:28
  133.1 6.3 %copy.46 = bf16[4,1024,512]{1,2,0:T(8,128)(2,1)} copy(bf16[4,1024,512]{2,1,0:T(8,128)(2,1)} %get-tuple-element.3) | data formatting | bytes 8388608
  139.4 0.0 copy-start.1
  139.4 0.0 copy-start.9
  139.4 3.5 %multiply_reduce_fusion = bf16[1024,8,64]{0,2,1:T(8,128)(2,1)S(1)} fusion(bf16[1024,8,4,64]{0,3,1,2:T(8,128)(2,1)} %bitcast.64, f32[1024,8,4]{0,1,2:T(8,128)S(1)} %bitcast_convert_fusion), kind=kLoop, calls=%fused_computation.6 | loop fusion | flops 5767168 | bytes 5373952 | tf_op jit(solution)/shard_map/krh,krhd->rhd/dot_general | solution.py:36
  142.9 0.0 copy-done.1
  142.9 0.0 copy-done.9
  142.9 2.6 %fusion.5 = bf16[1024,1024]{1,0:T(8,128)(2,1)} fusion(bf16[1024,1024]{1,0:T(8,128)(2,1)S(1)} %copy-done.1, bf16[1024,512]{0,1:T(8,128)(2,1)S(1)} %bitcast.67, bf16[512,1024]{1,0:T(8,128)(2,1)S(1)} %copy-done.9), kind=kOutput, calls=%fused_computation.14 | convolution fusion | flops 1076887552 | bytes 6291456 | tf_op jit(solution)/shard_map/dot_general | solution.py:87
  (15 shorter events, 0.2 us)
Async XLA Ops:
  0.6 12.9 %copy-start = (bf16[1024,1024]{1,0:T(8,128)(2,1)S(1)}, bf16[1024,1024]{1,0:T(8,128)(2,1)}, u32[]{:S(2)}) copy-start(bf16[1024,1024]{1,0:T(8,128)(2,1)} %param.22) | copy-start | bytes 6291460
  3.3 15.6 %all-to-all-start = ((s32[16,1,32]{2,1,0:T(1,128)}), s32[16,1,32]{2,1,0:T(1,128)S(1)}, u32[]{:S(2)}, u32[]{:S(2)}) async-start(s32[16,1,32]{2,1,0:T(1,128)} %all_to_all.11), calls=%async_computation | async-start | bytes 16384 | tf_op jit(solution)/shard_map/all_to_all | solution.py:61
  13.5 5.3 %copy-start.2 = (bf16[16,1024]{1,0:T(8,128)(2,1)S(1)}, bf16[16,1024]{1,0:T(8,128)(2,1)}, u32[]{:S(2)}) copy-start(bf16[16,1024]{1,0:T(8,128)(2,1)} %param.17) | copy-start | bytes 98308
  19.0 11.6 %copy-start.6 = (f32[1024]{0:T(1024)S(1)}, f32[1024]{0:T(1024)}, u32[]{:S(2)}) copy-start(f32[1024]{0:T(1024)} %param.19) | copy-start | bytes 12292
  19.0 13.2 %copy-start.4 = (s32[4,1024]{1,0:T(4,128)S(1)}, s32[4,1024]{1,0:T(4,128)}, u32[]{:S(2)}) copy-start(s32[4,1024]{1,0:T(4,128)} %param.31) | copy-start | bytes 49156
  19.1 13.2 %copy-start.5 = (s32[1,4096]{1,0:T(1,128)S(1)}, s32[1,4096]{1,0:T(1,128)}, u32[]{:S(2)}) copy-start(s32[1,4096]{1,0:T(1,128)} %param.30) | copy-start | bytes 49156
  24.4 35.7 %all-to-all-start.1 = ((bf16[16,32,1024]{2,1,0:T(8,128)(2,1)}), bf16[16,32,1024]{2,1,0:T(8,128)(2,1)S(1)}, u32[]{:S(2)}, u32[]{:S(2)}) async-start(bf16[16,32,1024]{2,1,0:T(8,128)(2,1)} %bitcast.66), calls=%async_computation.1 | async-start | bytes 2097152 | tf_op jit(solution)/shard_map/all_to_all | solution.py:65
  32.3 23.1 %copy-start.8 = (s32[16]{0:T(128)S(1)}, s32[16]{0:T(128)}, u32[]{:S(2)}) copy-start(s32[16]{0:T(128)} %param.29) | copy-start | bytes 196
  32.3 23.2 %copy-start.10 = (f32[1024]{0:T(1024)S(1)}, f32[1024]{0:T(1024)}, u32[]{:S(2)}) copy-start(f32[1024]{0:T(1024)} %param.18) | copy-start | bytes 12292
  64.2 8.9 %copy-start.7 = (f32[1024]{0:T(1024)S(1)}, f32[1024]{0:T(1024)}, u32[]{:S(2)}) copy-start(f32[1024]{0:T(1024)} %param.20) | copy-start | bytes 12292
  73.1 43.7 %copy-start.3 = (bf16[16,1024]{1,0:T(8,128)(2,1)}, bf16[16,1024]{1,0:T(8,128)(2,1)S(1)}, u32[]{:S(2)}) copy-start(bf16[16,1024]{1,0:T(8,128)(2,1)S(1)} %get-tuple-element.7) | copy-start | bytes 98308
  139.4 3.5 %copy-start.1 = (bf16[1024,1024]{1,0:T(8,128)(2,1)S(1)}, bf16[1024,1024]{1,0:T(8,128)(2,1)}, u32[]{:S(2)}) copy-start(bf16[1024,1024]{1,0:T(8,128)(2,1)} %param.16) | copy-start | bytes 6291460
  139.4 3.5 %copy-start.9 = (bf16[512,1024]{1,0:T(8,128)(2,1)S(1)}, bf16[512,1024]{1,0:T(8,128)(2,1)}, u32[]{:S(2)}) copy-start(bf16[512,1024]{1,0:T(8,128)(2,1)} %param.26) | copy-start | bytes 3145732
where the time goes:
time: 146 us
  local copies, waits for them, and re-layouts  73.9 us (51%)
  blocking collectives  23.4 us (16%)
  matrix products  21.5 us (15%)
  starting transfers between devices  13.4 us (9%)
  other arithmetic  12.3 us (8%)
    gather x3, local copies, waits for them, and re-layouts, on_device(): dec_keys = everyone[global_rows[dec_slot]]  41.3 us
    all_gather x1, blocking collectives, on_device(): everyone = lax.all_gather(latent_pairs, 'dom', axis=0, tiled=True)  23.4 us
    unnamed x25, local copies, waits for them, and re-layouts  13.2 us
    all_to_all x1, starting transfers between devices, on_device(): lax.all_to_all(requests, 'dom', split_axis=0, concat_axis=0, tiled=True)  7.41 us
    slice x2, local copies, waits for them, and re-layouts, attend_keys(): key_rows[..., :inner_width].reshape(edge_count, rows_here, HEADS, head_size)  7.01 us
    all_to_all x1, starting transfers between devices, on_device(): lax.all_to_all(source_rows[wanted], 'dom', split_axis=0, concat_axis=0, t...  6.01 us
    gather x1, local copies, waits for them, and re-layouts, on_device(): source_rows[wanted]  5.36 us
    dot_general x1, matrix products, on_device(): jnp.dot(normed_grid, w_kv_enc, preferred_element_type=jnp.float32)  5.3 us
  transfers between devices with their start and end apart: 2, of which 0 were waited for; matrix products, arithmetic and copies ran while one was open for 26% of the time, Pallas kernels for 0%

commit v1 on v0

v1 whole, which is shorter than its diff:
```python
import math

import jax
import jax.numpy as jnp
from jax import lax
from jax.sharding import PartitionSpec as P

HEADS = 8
norm_eps = 1e-06
F32 = jnp.float32
BF16 = jnp.bfloat16


def rms_norm(values, weight_gain):
    widened = values.astype(F32)
    spread = jnp.mean(widened * widened, axis=-1, keepdims=True)
    return (widened * lax.rsqrt(spread + norm_eps) * weight_gain).astype(BF16)


def attend_dense(queries, pairs, edges):
    rows, width = queries.shape
    head = width // HEADS
    q = queries.reshape(rows, HEADS, head)
    k = pairs[:, :width].reshape(-1, HEADS, head)
    v = pairs[:, width:].reshape(-1, HEADS, head)
    scores = jnp.einsum("rhd,khd->hrk", q, k, preferred_element_type=F32)
    scores = jnp.where(edges[None] > 0, scores * (1.0 / math.sqrt(head)), -1e30)
    highest = jnp.max(scores, axis=-1, keepdims=True)
    raised = jnp.exp(scores - highest) * edges[None]
    weights = (raised / jnp.sum(raised, axis=-1, keepdims=True)).astype(BF16)
    mixed = jnp.einsum("hrk,khd->rhd", weights, v, preferred_element_type=F32)
    return mixed.reshape(rows, width).astype(BF16)


def on_device(grid, latent_in, grid_gain, node_gain, dec_gain, w_q_enc, w_kv_enc, w_o_enc,
              w_q_dec, w_kv_dec, w_o_dec, enc_need, enc_slot, enc_count, dec_need, dec_slot):
    peers = lax.axis_size("dom")
    nodes = latent_in.shape[0]
    normed_grid = rms_norm(grid, grid_gain)
    wanted = lax.all_to_all(enc_need.reshape(peers, -1), "dom", split_axis=0, concat_axis=0, tiled=True)
    band = jnp.arange(grid.shape[0], dtype=jnp.int32)
    pick = (wanted.reshape(-1)[:, None] == band[None, :]).astype(BF16)
    chosen = jnp.dot(pick, normed_grid, preferred_element_type=F32).astype(BF16)
    rows = jnp.dot(chosen, w_kv_enc, preferred_element_type=F32).astype(BF16)
    arrived = lax.all_to_all(rows, "dom", split_axis=0, concat_axis=0, tiled=True)
    enc_queries = jnp.dot(rms_norm(latent_in, node_gain), w_q_enc, preferred_element_type=F32).astype(BF16)
    live = jnp.arange(enc_slot.shape[0], dtype=jnp.int32)[:, None] < enc_count[None, :]
    slot_row = jnp.arange(enc_need.shape[1], dtype=jnp.int32)
    enc_edges = jnp.sum((live[:, :, None] & (enc_slot[:, :, None] == slot_row)).astype(F32), axis=0)
    enc_mixed = attend_dense(enc_queries, arrived, enc_edges)
    enc_update = jnp.dot(enc_mixed, w_o_enc, preferred_element_type=F32)
    latent_out = (latent_in.astype(F32) + enc_update).astype(BF16)
    latent_pairs = jnp.dot(rms_norm(latent_out, dec_gain), w_kv_dec, preferred_element_type=F32).astype(BF16)
    dec_queries = jnp.dot(normed_grid, w_q_dec, preferred_element_type=F32).astype(BF16)
    everyone = lax.all_gather(latent_pairs, "dom", axis=0, tiled=True)
    total = dec_need.shape[1]
    cap = total // peers
    lanes = 128
    table = dec_need.reshape(total // lanes, lanes).astype(BF16)
    high = (dec_slot // lanes)[:, :, None] == jnp.arange(total // lanes, dtype=jnp.int32)
    low = (dec_slot % lanes)[:, :, None] == jnp.arange(lanes, dtype=jnp.int32)
    need = jnp.einsum("jgt,tl->jgl", high.astype(BF16), table, preferred_element_type=F32)
    need = jnp.sum(jnp.where(low, need, 0.0), axis=-1).astype(jnp.int32)
    node = (dec_slot // cap) * nodes + need
    dec_edges = jnp.sum((node[:, :, None] == jnp.arange(peers * nodes, dtype=jnp.int32)).astype(F32), axis=0)
    dec_mixed = attend_dense(dec_queries, everyone, dec_edges)
    dec_update = jnp.dot(dec_mixed, w_o_dec, preferred_element_type=F32)
    grid_out = (grid.astype(F32) + dec_update).astype(BF16)
    return (latent_out, grid_out)


def solution(mesh):
    both, rep = P(("groups", "dom"), None), P()
    return jax.shard_map(
        on_device,
        mesh=mesh,
        in_specs=(both, both, *([rep] * 9), P("dom", None), P(None, "dom"), P("dom"), P("dom", None), P(None, "dom")),
        out_specs=(both, both),
        check_vma=False,
    )
```

time: 146 us -> 103 us (0.71)
  local copies, waits for them, and re-layouts: 73.9 us -> 11.6 us
  waiting for transfers between devices: 0.01 us -> 13.8 us
  matrix products: 21.5 us -> 30.8 us
  other arithmetic: 12.3 us -> 8.05 us
    gather x5 -> x0, local copies, waits for them, and re-layouts: 49.5 us -> none  [the longest x3 41.3 us: on_device(): dec_keys = everyone[global_rows[dec_slot]]]
    all_to_all x2, waiting for transfers between devices: 0.01 us -> 13.8 us  [the longest x1 13.6 us: on_device(): lax.all_to_all(rows, 'dom', split_axis=0, concat_axis=0, tiled=True)]
    unnamed x25 -> x26, local copies, waits for them, and re-layouts: 13.2 us -> 2.8 us
    sub x0 -> x1, matrix products: none -> 8.1 us  [attend_dense(): raised = jnp.exp(scores - highest) * edges[None]]
    dot_general x2 -> x0, other arithmetic: 7.57 us -> none  [the longest x1 4.1 us: attend_keys(): jnp.einsum('rhd,krhd->krh', query_heads, key_heads, preferred_element_typ...]
    reshape x3 -> x1, local copies, waits for them, and re-layouts: 3.22 us -> 0.09 us  [attend_dense(): q = queries.reshape(rows, HEADS, head)]
    reduce_sum x1 -> x2, other arithmetic: 0.03 us -> 1.76 us  [the longest x1 1.52 us: on_device(): jnp.sum((node[:, :, None] == jnp.arange(peers * nodes, dtype=jnp.int32))....]
    slice x2 -> x4, local copies, waits for them, and re-layouts: 7.01 us -> 5.44 us  [the longest x3 4.6 us: attend_dense(): k = pairs[:, :width].reshape(-1, HEADS, head)]
  transfers between devices with their start and end apart: 2 -> 2, of which waited for: 0 -> 2; matrix products, arithmetic and copies ran while one was open for 26% -> 15% of each run, Pallas kernels for 0% -> 0%
where the time goes in v1:
time: 103 us
  matrix products  30.8 us (30%)
  blocking collectives  24.2 us (23%)
  waiting for transfers between devices  13.8 us (13%)
  starting transfers between devices  13.4 us (13%)
  local copies, waits for them, and re-layouts  11.6 us (11%)
  other arithmetic  8.05 us (8%)
    all_gather x1, blocking collectives, on_device(): everyone = lax.all_gather(latent_pairs, 'dom', axis=0, tiled=True)  24.2 us
    all_to_all x1, waiting for transfers between devices, on_device(): lax.all_to_all(rows, 'dom', split_axis=0, concat_axis=0, tiled=True)  13.6 us
    sub x1, matrix products, attend_dense(): raised = jnp.exp(scores - highest) * edges[None]  8.1 us
    all_to_all x1, starting transfers between devices, on_device(): lax.all_to_all(enc_need.reshape(peers, -1), 'dom', split_axis=0, concat_a...  7.41 us
    all_to_all x1, starting transfers between devices, on_device(): lax.all_to_all(rows, 'dom', split_axis=0, concat_axis=0, tiled=True)  6 us
    dot_general x1, matrix products, on_device(): rows = jnp.dot(chosen, w_kv_enc, preferred_element_type=F32).astype(BF16)  5.09 us
    dot_general x2, matrix products, attend_dense(): mixed = jnp.einsum('hrk,khd->rhd', weights, v, preferred_element_type=F32)  4.7 us
    slice x3, local copies, waits for them, and re-layouts, attend_dense(): k = pairs[:, :width].reshape(-1, HEADS, head)  4.6 us
  transfers between devices with their start and end apart: 2, of which 2 were waited for; matrix products, arithmetic and copies ran while one was open for 15% of the time, Pallas kernels for 0%

profile of v1, /device:TPU:0, one launch (start us, length us, event | category | flops | bytes accessed | tf_op | source)
XLA Modules:
  0.0 102.7 jit_solution(15868133471718413483)
XLA Ops:
  0.6 0.0 copy-start
  0.6 0.5 broadcast.115
  1.2 1.5 %reduce.8 = s32[512]{0:T(512)S(1)} reduce(s32[1,512]{1,0:T(1,128)} %param.27, s32[]{:T(128)} %broadcast.115), dimensions={0}, to_apply=%param.27.reduce_sub_computation.3 | reduce | bytes 4100 | tf_op args[11]
  2.6 0.7 all_to_all.14
  3.3 7.4 %all-to-all-start = ((s32[16,1,32]{2,1,0:T(1,128)}), s32[16,1,32]{2,1,0:T(1,128)S(1)}, u32[]{:S(2)}, u32[]{:S(2)}) async-start(s32[16,1,32]{2,1,0:T(1,128)} %all_to_all.14), calls=%async_computation | async-start | bytes 16384 | tf_op jit(solution)/shard_map/all_to_all | solution.py:40
  10.7 0.9 fusion.32
  11.6 2.1 %fusion.3 = f32[1024]{0:T(1024)S(1)} fusion(bf16[1024,1024]{1,0:T(8,128)(2,1)} %param.16), kind=kLoop, calls=%fused_computation.9 | loop fusion | flops 3144704 | bytes 2101248 | tf_op jit(solution)/shard_map/reduce_sum | solution.py:16
  13.7 1.5 %convolution_convert_fusion.4 = bf16[16,512]{1,0:T(8,128)(2,1)S(1)} fusion(bf16[1024,512]{1,0:T(8,128)(2,1)} %param.21, bf16[16,1024]{1,0:T(8,128)(2,1)} %param.17, f32[1024]{0:T(1024)} %param.19, f32[16]{0:T(128)S(1)} %add_rsqrt_fusion.2), kind=kOutput, calls=%fused_computation.37 | convolution fusion | flops 16850944 | bytes 1101888 | tf_op jit(solution)/shard_map/dot_general | solution.py:46
  15.2 0.8 convert_reduce_fusion.2
  16.0 0.1 reshape.100
  16.1 0.8 copy.42
  16.9 0.2 all-to-all-done
  17.1 0.7 reduce.9
  17.8 0.1 eq.34
  17.8 0.0 copy-done
  17.8 0.0 copy-start.6
  17.8 5.1 %convolution_convert_fusion.1 = bf16[512,1024]{1,0:T(8,128)(2,1)} fusion(bf16[1024,1024]{1,0:T(8,128)(2,1)S(1)} %copy-done, s32[512]{0:T(512)S(1)} %eq.34, bf16[1024,1024]{1,0:T(8,128)(2,1)} %param.16, f32[1024]{0:T(1024)} %param.18, f32[1024]{0:T(1024)S(1)} %add_rsqrt_fusion), kind=kOutput, calls=%fused_computation.26 | convolution fusion | flops 2153250816 | bytes 5253120 | tf_op jit(solution)/shard_map/dot_general | solution.py:44
  22.9 0.0 copy-start.8
  22.9 0.0 copy-start.10
  22.9 6.0 %all-to-all-start.1 = ((bf16[16,32,1024]{2,1,0:T(8,128)(2,1)}), bf16[16,32,1024]{2,1,0:T(8,128)(2,1)}, u32[]{:S(2)}, u32[]{:S(2)}) async-start(bf16[16,32,1024]{2,1,0:T(8,128)(2,1)} %bitcast), calls=%async_computation.1 | async-start | bytes 2097152 | tf_op jit(solution)/shard_map/all_to_all | solution.py:45
  28.9 0.0 copy-done.6
  29.0 0.6 select_reduce_fusion
  29.6 1.5 %convert_reduce_fusion = f32[1024,256]{1,0:T(8,128)S(1)} fusion(s32[4,1024]{1,0:T(4,128)S(1)} %fusion.44), kind=kLoop, calls=%fused_computation.15 | loop fusion | flops 2883584 | bytes 1064960 | tf_op jit(solution)/shard_map/reduce_sum | solution.py:65
  31.1 1.3 %copy.49 = f32[1024,256]{0,1:T(8,128)} copy(f32[1024,256]{1,0:T(8,128)S(1)} %convert_reduce_fusion) | data formatting | bytes 2097152 | tf_op jit(solution)/shard_map/reduce_sum | solution.py:65
  32.4 0.1 broadcast_compare_fusion
  32.6 1.1 %copy.47 = pred[1024,256]{0,1:T(8,128)(4,1)} copy(pred[1024,256]{1,0:T(8,128)(4,1)S(1)} %broadcast_compare_fusion) | data formatting | bytes 524288 | tf_op jit(solution)/shard_map/gt | solution.py:27
  33.6 0.0 copy-done.8
  33.7 0.2 convert_reduce_fusion.1
  33.9 0.0 copy-done.10
  33.9 4.3 %convolution_convert_fusion = bf16[1024,512]{0,1:T(8,128)(2,1)} fusion(bf16[1024,512]{1,0:T(8,128)(2,1)} %param.24, bf16[1024,1024]{1,0:T(8,128)(2,1)} %param.16, f32[1024]{0:T(1024)S(1)} %copy-done.10, f32[1024]{0:T(1024)S(1)} %add_rsqrt_fusion), kind=kOutput, calls=%fused_computation.25 | convolution fusion | flops 1078460416 | bytes 4202496 | tf_op jit(solution)/shard_map/dot_general | solution.py:54
  38.3 0.0 copy-start.3
  38.3 0.0 copy-start.7
  38.3 13.6 %all-to-all-done.1 = bf16[16,32,1024]{2,1,0:T(8,128)(2,1)} async-done(((bf16[16,32,1024]{2,1,0:T(8,128)(2,1)}), bf16[16,32,1024]{2,1,0:T(8,128)(2,1)}, u32[]{:S(2)}, u32[]{:S(2)}) %all-to-all-start.1) | async-done | bytes 1048608 | tf_op jit(solution)/shard_map/all_to_all | solution.py:45
  51.9 2.1 %fusion.49 = (bf16[512,512]{1,0:T(8,128)(2,1)}, bf16[512,512]{1,0:T(8,128)(2,1)S(1)}) fusion(bf16[512,1024]{1,0:T(8,128)(2,1)} %bitcast.1), kind=kLoop, calls=%fused_computation.86 | loop fusion | bytes 2097152 | tf_op jit(solution)/shard_map/slice | solution.py:24
  54.0 1.3 %copy.53 = bf16[512,512]{0,1:T(8,128)(2,1)S(1)} copy(bf16[512,512]{1,0:T(8,128)(2,1)} %get-tuple-element.2) | data formatting | bytes 1048576
  55.2 0.2 fusion.15
  55.4 0.2 fusion.51
  55.6 0.2 copy.52
  55.8 0.3 fusion.19
  56.1 0.0 copy-start.2
  56.2 0.1 convert_element_type.93
  56.3 0.0 copy-done.3
  56.3 1.7 %fusion.29 = (f32[16]{0:T(128)S(1)}, bf16[16,1024]{1,0:T(8,128)(2,1)S(1)}) fusion(bf16[16,512]{1,0:T(8,128)(2,1)S(1)} %convert_element_type.93, bf16[512,1024]{1,0:T(8,128)(2,1)} %param.23, bf16[16,1024]{1,0:T(8,128)(2,1)S(1)} %copy-done.3), kind=kOutput, calls=%fused_computation.52 | convolution fusion | flops 16875504 | bytes 1130560 | tf_op jit(solution)/shard_map/dot_general | solution.py:51
  57.9 0.0 copy-start.5
  58.0 0.0 copy-done.7
  58.0 2.0 %convolution_convert_fusion.2 = bf16[16,1024]{1,0:T(8,128)(2,1)S(1)} fusion(bf16[1024,1024]{1,0:T(8,128)(2,1)} %param.25, bf16[16,1024]{1,0:T(8,128)(2,1)S(1)} %get-tuple-element.9, f32[1024]{0:T(1024)S(1)} %copy-done.7, f32[16]{0:T(128)S(1)} %add_rsqrt_fusion.1), kind=kOutput, calls=%fused_computation.34 | convolution fusion | flops 33636352 | bytes 2166848 | tf_op jit(solution)/shard_map/dot_general | solution.py:53
  60.0 24.2 %all_gather.3 = bf16[256,1024]{1,0:T(8,128)(2,1)S(1)} all-gather(bf16[16,1024]{1,0:T(8,128)(2,1)S(1)} %convolution_convert_fusion.2), channel_id=1, replica_groups=mesh['groups'=2,'dom'=16] {'dom'}, dimensions={0}, use_global_device_ids=true | all-gather | bytes 557056 | tf_op jit(solution)/shard_map/all_gather | solution.py:55
  84.2 0.7 fusion.50
  84.9 1.8 %copy.48 = bf16[256,512]{0,1:T(8,128)(2,1)} copy(bf16[256,512]{1,0:T(8,128)(2,1)} %get-tuple-element.4) | data formatting | bytes 524288 | tf_op jit(solution)/shard_map/slice | solution.py:24
  86.7 0.8 copy.46
  87.6 0.0 copy-done.2
  87.6 0.0 copy-start.4
  87.6 8.1 %fusion.52 = (f32[8,1024]{1,0:T(8,128)S(1)}, f32[8,1024,256]{1,2,0:T(8,128)}) fusion(f32[1024,256]{0,1:T(8,128)S(1)} %copy-done.2, pred[1024,256]{0,1:T(8,128)(4,1)} %copy.47, bf16[1024,8,64]{0,2,1:T(8,128)(2,1)} %bitcast.36, bf16[256,8,64]{0,2,1:T(8,128)(2,1)} %bitcast.34), kind=kOutput, calls=%fused_computation.89 | convolution fusion | flops 278921472 | bytes 11042816 | tf_op jit(solution)/shard_map/sub | solution.py:29
  95.7 0.0 copy-done.5
  95.7 0.0 copy-done.4
  95.7 0.0 copy-start.1
  95.7 0.0 copy-start.9
  95.7 4.4 %fusion.12 = bf16[8,64,1024]{2,1,0:T(8,128)(2,1)S(1)} fusion(bf16[256,8,64]{0,2,1:T(8,128)(2,1)S(1)} %bitcast.35, f32[8,1024,256]{1,2,0:T(8,128)} %get-tuple-element.11, f32[8,1024]{1,0:T(8,128)S(1)} %get-tuple-element.10), kind=kOutput, calls=%fused_computation.23 | convolution fusion | flops 273154048 | bytes 9732096 | tf_op jit(solution)/shard_map/hrk,khd->rhd/dot_general | solution.py:31
  100.1 0.0 copy-done.1
  100.1 0.0 copy-done.9
  100.1 2.6 %fusion.6 = bf16[1024,1024]{1,0:T(8,128)(2,1)} fusion(bf16[1024,1024]{1,0:T(8,128)(2,1)S(1)} %copy-done.1, bf16[1024,512]{0,1:T(8,128)(2,1)S(1)} %bitcast.37, bf16[512,1024]{1,0:T(8,128)(2,1)S(1)} %copy-done.9), kind=kOutput, calls=%fused_computation.12 | convolution fusion | flops 1076887552 | bytes 6291456 | tf_op jit(solution)/shard_map/dot_general | solution.py:67
  (8 shorter events, 0.1 us)
Async XLA Ops:
  0.6 17.2 %copy-start = (bf16[1024,1024]{1,0:T(8,128)(2,1)S(1)}, bf16[1024,1024]{1,0:T(8,128)(2,1)}, u32[]{:S(2)}) copy-start(bf16[1024,1024]{1,0:T(8,128)(2,1)} %param.22) | copy-start | bytes 6291460
  3.3 13.8 %all-to-all-start = ((s32[16,1,32]{2,1,0:T(1,128)}), s32[16,1,32]{2,1,0:T(1,128)S(1)}, u32[]{:S(2)}, u32[]{:S(2)}) async-start(s32[16,1,32]{2,1,0:T(1,128)} %all_to_all.14), calls=%async_computation | async-start | bytes 16384 | tf_op jit(solution)/shard_map/all_to_all | solution.py:40
  17.8 11.1 %copy-start.6 = (s32[4,1024]{1,0:T(4,128)S(1)}, s32[4,1024]{1,0:T(4,128)}, u32[]{:S(2)}) copy-start(s32[4,1024]{1,0:T(4,128)} %param.31) | copy-start | bytes 49156
  22.9 10.7 %copy-start.8 = (s32[16]{0:T(128)S(1)}, s32[16]{0:T(128)}, u32[]{:S(2)}) copy-start(s32[16]{0:T(128)} %param.29) | copy-start | bytes 196
  22.9 11.0 %copy-start.10 = (f32[1024]{0:T(1024)S(1)}, f32[1024]{0:T(1024)}, u32[]{:S(2)}) copy-start(f32[1024]{0:T(1024)} %param.18) | copy-start | bytes 12292
  22.9 29.0 %all-to-all-start.1 = ((bf16[16,32,1024]{2,1,0:T(8,128)(2,1)}), bf16[16,32,1024]{2,1,0:T(8,128)(2,1)}, u32[]{:S(2)}, u32[]{:S(2)}) async-start(bf16[16,32,1024]{2,1,0:T(8,128)(2,1)} %bitcast), calls=%async_computation.1 | async-start | bytes 2097152 | tf_op jit(solution)/shard_map/all_to_all | solution.py:45
  38.3 18.0 %copy-start.3 = (bf16[16,1024]{1,0:T(8,128)(2,1)S(1)}, bf16[16,1024]{1,0:T(8,128)(2,1)}, u32[]{:S(2)}) copy-start(bf16[16,1024]{1,0:T(8,128)(2,1)} %param.17) | copy-start | bytes 98308
  38.3 19.7 %copy-start.7 = (f32[1024]{0:T(1024)S(1)}, f32[1024]{0:T(1024)}, u32[]{:S(2)}) copy-start(f32[1024]{0:T(1024)} %param.20) | copy-start | bytes 12292
  56.1 31.4 %copy-start.2 = (f32[1024,256]{0,1:T(8,128)S(1)}, f32[1024,256]{0,1:T(8,128)}, u32[]{:S(2)}) copy-start(f32[1024,256]{0,1:T(8,128)} %copy.49) | copy-start | bytes 3145732
  57.9 37.7 %copy-start.5 = (bf16[16,1024]{1,0:T(8,128)(2,1)}, bf16[16,1024]{1,0:T(8,128)(2,1)S(1)}, u32[]{:S(2)}) copy-start(bf16[16,1024]{1,0:T(8,128)(2,1)S(1)} %get-tuple-element.9) | copy-start | bytes 98308
  87.6 8.1 %copy-start.4 = (bf16[256,512]{0,1:T(8,128)(2,1)S(1)}, bf16[256,512]{0,1:T(8,128)(2,1)}, u32[]{:S(2)}) copy-start(bf16[256,512]{0,1:T(8,128)(2,1)} %copy.46) | copy-start | bytes 786436
  95.7 4.4 %copy-start.1 = (bf16[1024,1024]{1,0:T(8,128)(2,1)S(1)}, bf16[1024,1024]{1,0:T(8,128)(2,1)}, u32[]{:S(2)}) copy-start(bf16[1024,1024]{1,0:T(8,128)(2,1)} %param.16) | copy-start | bytes 6291460
  95.7 4.4 %copy-start.9 = (bf16[512,1024]{1,0:T(8,128)(2,1)S(1)}, bf16[512,1024]{1,0:T(8,128)(2,1)}, u32[]{:S(2)}) copy-start(bf16[512,1024]{1,0:T(8,128)(2,1)} %param.26) | copy-start | bytes 3145732

commit v2 on v1

--- a/solution.py
+++ b/solution.py
@@ -1,8 +1,11 @@
+import functools
 import math
 
 import jax
 import jax.numpy as jnp
 from jax import lax
+from jax.experimental import pallas as pl
+from jax.experimental.pallas import tpu as pltpu
 from jax.sharding import PartitionSpec as P
 
 HEADS = 8
@@ -69,10 +72,346 @@
     return (latent_out, grid_out)
 
 
+NT = (((1,), (1,)), ((), ()))
+TN = (((0,), (0,)), ((), ()))
+HIGH = lax.Precision.HIGHEST
+
+
+def iota(shape, dim):
+    return lax.broadcasted_iota(jnp.int32, shape, dim)
+
+
+def norm_into(values, gain):
+    widened = values.astype(F32)
+    spread = jnp.mean(widened * widened, axis=-1, keepdims=True)
+    return (widened * lax.rsqrt(spread + norm_eps) * gain).astype(BF16)
+
+
+def encoder_kernel(
+    peers, grid_hbm, latent_ref, ggain_ref, ngain_ref, dgain_ref, wq_hbm, wkv_hbm, wo_hbm, wqd_hbm, wkvd_hbm,
+    need_ref, slot_ref, count_ref,
+    latent_out, pairs_out, queries_out,
+    grid_v, wq_v, wkv_v, wo_v, wqd_v, wkvd_v, normed, rows, query_mine, edges_mine,
+    need_all, query_all, edges_all, mix_send, stat_send, mix_all, stat_all, pairs_all,
+    load_sem, send_sem, recv_sem,
+):
+    me = lax.axis_index("dom")
+    nodes, model = latent_ref.shape
+    width = wq_v.shape[1]
+    head = width // HEADS
+    cap = edges_all.shape[1]
+    points = grid_v.shape[0]
+    lanes = HEADS * nodes
+
+    loads = [
+        pltpu.make_async_copy(source, target, load_sem.at[number])
+        for number, (source, target) in enumerate(
+            ((wq_hbm, wq_v), (grid_hbm, grid_v), (wkv_hbm, wkv_v), (wqd_hbm, wqd_v), (wo_hbm, wo_v), (wkvd_hbm, wkvd_v))
+        )
+    ]
+    for load in loads:
+        load.start()
+
+    barrier = pltpu.get_barrier_semaphore()
+    for step in range(1, peers):
+        pl.semaphore_signal(
+            barrier, inc=1, device_id={"dom": lax.rem(me + step, peers)}, device_id_type=pl.DeviceIdType.MESH
+        )
+
+    def message(kind, source, target, to, slot):
+        return pltpu.make_async_remote_copy(
+            src_ref=source,
+            dst_ref=target,
+            send_sem=send_sem.at[kind, to],
+            recv_sem=recv_sem.at[kind, slot],
+            device_id={"dom": to},
+            device_id_type=pl.DeviceIdType.MESH,
+        )
+
+    def need_to(to, slot):
+        return message(0, need_ref, need_all.at[slot], to, slot)
+
+    def query_to(to, slot):
+        return message(1, query_mine, query_all.at[slot], to, slot)
+
+    def edges_to(to, slot):
+        return message(2, edges_mine.at[to], edges_all.at[slot], to, slot)
+
+    def mix_to(to, slot):
+        return message(3, mix_send.at[to], mix_all.at[slot], to, slot)
+
+    def stat_to(to, slot):
+        return message(4, stat_send.at[to], stat_all.at[slot], to, slot)
+
+    def pairs_to(to, slot):
+        return message(5, pairs_all.at[me], pairs_all.at[slot], to, slot)
+
+    def each_peer(act):
+        def body(step, carry):
+            act(lax.rem(me + step, peers))
+            return carry
+
+        lax.fori_loop(1, peers, body, 0)
+
+    pl.semaphore_wait(barrier, peers - 1)
+    each_peer(lambda to: need_to(to, me).start())
+    need_all[me] = need_ref[...]
+
+    loads[0].wait()
+    queries = jnp.dot(
+        norm_into(latent_ref[...], ngain_ref[...]), wq_v[...], preferred_element_type=F32
+    ).astype(BF16)
+    query_mine[...] = queries
+    query_all[me] = queries
+    each_peer(lambda to: query_to(to, me).start())
+
+    edge_total = slot_ref.shape[0]
+    slots = jnp.where(iota(slot_ref.shape, 0) < count_ref[...], slot_ref[...], -1).astype(F32)
+    turn = (iota((edge_total, edge_total), 0) == iota((edge_total, edge_total), 1)).astype(F32)
+    by_node = lax.dot_general(slots, turn, TN, precision=HIGH, preferred_element_type=F32)
+    entry = iota((nodes, peers * cap), 1).astype(F32)
+    tally = jnp.zeros((nodes, peers * cap), F32)
+    for j in range(edge_total):
+        tally = tally + jnp.where(by_node[:, j : j + 1] == entry, 1.0, 0.0)
+    spread_out = (iota((nodes, lanes), 0) == lax.rem(iota((nodes, lanes), 1), nodes)).astype(BF16)
+    tally = lax.dot_general(tally.astype(BF16), spread_out, TN, preferred_element_type=F32)
+    edges_mine[...] = tally.astype(BF16).reshape(peers, cap, lanes)
+    edges_all[me] = edges_mine[me]
+    each_peer(lambda to: edges_to(to, me).start())
+
+    loads[1].wait()
+
+    def norm_block(block, carry):
+        at = pl.ds(pl.multiple_of(block * 128, 128), 128)
+        normed[at, :] = norm_into(grid_v[at, :], ggain_ref[...])
+        return carry
+
+    lax.fori_loop(0, points // 128, norm_block, 0)
+
+    each_peer(lambda peer: need_to(peer, peer).wait_recv())
+    lists = need_all[...]
+    asked = jnp.broadcast_to(lists, (peers, cap, peers * cap))
+    mine = iota((peers, cap, peers * cap), 2) == me * cap + iota((peers, cap, peers * cap), 1)
+    wanted = jnp.sum(jnp.where(mine, asked.astype(F32), 0.0), axis=2, keepdims=True).astype(jnp.int32)
+    wanted = wanted.reshape(peers * cap, 1)
+    pick = jnp.where(wanted == iota((peers * cap, points), 1), 1.0, 0.0).astype(BF16)
+    chosen = jnp.dot(pick, normed[...], preferred_element_type=F32).astype(BF16)
+    loads[2].wait()
+    rows[...] = jnp.dot(chosen, wkv_v[...], preferred_element_type=F32).astype(BF16)
+
+    own_head = iota((lanes, width), 0) // nodes == iota((lanes, width), 1) // head
+
+    def window(w):
+        spread_query = jnp.broadcast_to(query_all[w][None], (HEADS, nodes, width)).reshape(lanes, width)
+        spread_query = jnp.where(own_head, spread_query, jnp.zeros_like(spread_query))
+        here = pl.ds(pl.multiple_of(w * cap, cap), cap)
+        scores = lax.dot_general(rows[here, :width], spread_query, NT, preferred_element_type=F32)
+        times = edges_all[w].astype(F32)
+        scores = jnp.where(times > 0, scores * (1.0 / math.sqrt(head)), -1e30)
+        highest = jnp.max(scores, axis=0, keepdims=True)
+        raised = jnp.exp(scores - highest) * times
+        total = jnp.sum(raised, axis=0, keepdims=True)
+        mixed = lax.dot_general(raised.astype(BF16), rows[here, width:], TN, preferred_element_type=F32)
+        mixed = jnp.where(own_head, mixed, 0.0).reshape(HEADS, nodes, width)
+        return jnp.sum(mixed, axis=0).astype(BF16), highest, total
+
+    def serve(peer):
+        query_to(peer, peer).wait_recv()
+        edges_to(peer, peer).wait_recv()
+        mixed, highest, total = window(peer)
+        mix_send[peer] = mixed
+        stat_send[peer, 0:1, :] = highest
+        stat_send[peer, 1:2, :] = total
+        mix_to(peer, me).start()
+        stat_to(peer, me).start()
+
+    each_peer(serve)
+    mixed, highest, total = window(me)
+    mix_all[me] = mixed
+    stat_all[me, 0:1, :] = highest
+    stat_all[me, 1:2, :] = total
+
+    loads[3].wait()
+    queries_out[...] = jnp.dot(normed[...], wqd_v[...], preferred_element_type=F32).astype(BF16)
+
+    def take_mix(peer):
+        mix_to(peer, peer).wait_recv()
+        stat_to(peer, peer).wait_recv()
+
+    each_peer(take_mix)
+    tops = [stat_all[peer, 0:1, :] for peer in range(peers)]
+    sums = [stat_all[peer, 1:2, :] for peer in range(peers)]
+    top = functools.reduce(jnp.maximum, tops)
+    shares = [jnp.exp(one - top) for one in tops]
+    whole = functools.reduce(jnp.add, [a * b for a, b in zip(shares, sums)])
+    own_node = iota((nodes, lanes), 0) == lax.rem(iota((nodes, lanes), 1), nodes)
+    stacked = jnp.concatenate([jnp.where(own_node, share / whole, 0.0) for share in shares], axis=0)
+    widen = (iota((lanes, width), 0) // nodes == iota((lanes, width), 1) // head).astype(F32)
+    factors = jnp.dot(stacked, widen, precision=HIGH, preferred_element_type=F32).reshape(peers, nodes, width)
+    enc_mixed = jnp.sum(factors * mix_all[...].astype(F32), axis=0).astype(BF16)
+    loads[4].wait()
+    update = jnp.dot(enc_mixed, wo_v[...], preferred_element_type=F32)
+    fresh = (latent_ref[...].astype(F32) + update).astype(BF16)
+    latent_out[...] = fresh
+    loads[5].wait()
+    pairs = jnp.dot(norm_into(fresh, dgain_ref[...]), wkvd_v[...], preferred_element_type=F32).astype(BF16)
+    pairs_all[me] = pairs
+    each_peer(lambda to: pairs_to(to, me).start())
+    each_peer(lambda peer: pairs_to(peer, peer).wait_recv())
+    pairs_out[...] = pairs_all[...].reshape(peers * nodes, model)
+
+    def drain(to):
+        for outgoing in (need_to, query_to, edges_to, mix_to, stat_to, pairs_to):
+            outgoing(to, me).wait_send()
+
+    each_peer(drain)
+
+
+def encode(grid, latent_in, grid_gain, node_gain, dec_gain, w_q_enc, w_kv_enc, w_o_enc, w_q_dec, w_kv_dec,
+           enc_need, enc_slot, enc_count):
+    peers = lax.axis_size("dom")
+    nodes, model = latent_in.shape
+    width = w_q_enc.shape[1]
+    entries = enc_need.shape[1]
+    cap = entries // peers
+    points = grid.shape[0]
+    vmem = pl.BlockSpec(memory_space=pltpu.VMEM)
+    far = pl.BlockSpec(memory_space=pl.ANY)
+    return pl.pallas_call(
+        functools.partial(encoder_kernel, peers),
+        name="encode",
+        out_shape=(
+            jax.ShapeDtypeStruct((nodes, model), BF16),
+            jax.ShapeDtypeStruct((peers * nodes, 2 * width), BF16),
+            jax.ShapeDtypeStruct((points, width), BF16),
+        ),
+        in_specs=[far, vmem, vmem, vmem, vmem, far, far, far, far, far, vmem, vmem, vmem],
+        out_specs=(vmem, vmem, vmem),
+        scratch_shapes=[
+            pltpu.VMEM(grid.shape, BF16),
+            pltpu.VMEM(w_q_enc.shape, BF16),
+            pltpu.VMEM(w_kv_enc.shape, BF16),
+            pltpu.VMEM(w_o_enc.shape, BF16),
+            pltpu.VMEM(w_q_dec.shape, BF16),
+            pltpu.VMEM(w_kv_dec.shape, BF16),
+            pltpu.VMEM(grid.shape, BF16),
+            pltpu.VMEM((entries, 2 * width), BF16),
+            pltpu.VMEM((nodes, width), BF16),
+            pltpu.VMEM((peers, cap, HEADS * nodes), BF16),
+            pltpu.VMEM((peers, 1, entries), jnp.int32),
+            pltpu.VMEM((peers, nodes, width), BF16),
+            pltpu.VMEM((peers, cap, HEADS * nodes), BF16),
+            pltpu.VMEM((peers, nodes, width), BF16),
+            pltpu.VMEM((peers, 2, HEADS * nodes), F32),
+            pltpu.VMEM((peers, nodes, width), BF16),
+            pltpu.VMEM((peers, 2, HEADS * nodes), F32),
+            pltpu.VMEM((peers, nodes, 2 * width), BF16),
+            pltpu.SemaphoreType.DMA((6,)),
+            pltpu.SemaphoreType.DMA((6, peers)),
+            pltpu.SemaphoreType.DMA((6, peers)),
+        ],
+        compiler_params=pltpu.CompilerParams(
+            collective_id=0, has_side_effects=True, vmem_limit_bytes=60 * 1024 * 1024
+        ),
+    )(grid, latent_in, grid_gain[None], node_gain[None], dec_gain[None], w_q_enc, w_kv_enc, w_o_enc, w_q_dec,
+      w_kv_dec, enc_need, enc_slot, enc_count[None])
+
+
+def decoder_kernel(cap, nodes, query_ref, pairs_ref, slot_ref, table_ref, grid_ref, wo_ref, out_ref, turned, mixed):
+    tile, width = query_ref.shape
+    head = width // HEADS
+    keys = pairs_ref.shape[0]
+
+    @pl.when(pl.program_id(0) == 0)
+    def _():
+        turned[...] = pairs_ref[:, width:].astype(F32).T.astype(BF16)
+
+    slots = slot_ref[...]
+    edge_total = slots.shape[0]
+    slots = jnp.concatenate([slots] * (8 // edge_total), axis=0)
+    columns = []
+    for part in range(tile // 128):
+        piece = slots[:, part * 128 : (part + 1) * 128]
+        high = piece // 128
+        low = lax.rem(piece, 128)
+        need = jnp.zeros_like(piece)
+        for line in range(table_ref.shape[0]):
+            entry = jnp.broadcast_to(table_ref[line : line + 1, :], piece.shape)
+            need = jnp.where(high == line, jnp.take_along_axis(entry, low, axis=1), need)
+        columns.append((piece // cap) * nodes + need)
+    node = jnp.concatenate(columns, axis=1)
+    name = iota((keys, tile), 0)
+    times = jnp.zeros((keys, tile), F32)
+    for j in range(edge_total):
+        times = times + jnp.where(node[j : j + 1, :] == name, 1.0, 0.0)
+    bias = jnp.where(times > 0, jnp.log(jnp.maximum(times, 1.0)), -1e30)
+    lanes_of = iota((keys, 2 * head), 1) // head
+    for pair in range(HEADS // 2):
+        at = slice(pair * 2 * head, (pair + 1) * 2 * head)
+        query = query_ref[:, at]
+        key = pairs_ref[:, at] * (1.0 / math.sqrt(head))
+        for side in range(2):
+            h = pair * 2 + side
+            own = jnp.where(lanes_of == side, key, jnp.zeros_like(key))
+            scores = lax.dot_general(own, query, NT, preferred_element_type=F32) + bias
+            highest = jnp.max(scores, axis=0, keepdims=True)
+            raised = jnp.exp(scores - highest)
+            total = jnp.sum(raised, axis=0, keepdims=True)
+            got = jnp.dot(turned[h * head : (h + 1) * head, :], raised.astype(BF16), preferred_element_type=F32)
+            mixed[h * head : (h + 1) * head, :] = (got / total).astype(BF16)
+    update = lax.dot_general(mixed[...], wo_ref[...], TN, preferred_element_type=F32)
+    out_ref[...] = (grid_ref[...].astype(F32) + update).astype(BF16)
+
+
+def decode(queries, pairs, dec_slot, dec_need, grid, w_o_dec, nodes):
+    peers = lax.axis_size("dom")
+    points, model = grid.shape
+    width = queries.shape[1]
+    tile = 256
+    table = dec_need.reshape(-1, 128)
+    whole = lambda shape: pl.BlockSpec(shape, lambda i: (0, 0))
+    return pl.pallas_call(
+        functools.partial(decoder_kernel, dec_need.shape[1] // peers, nodes),
+        name="decode",
+        grid=(points // tile,),
+        out_shape=jax.ShapeDtypeStruct(grid.shape, BF16),
+        in_specs=[
+            pl.BlockSpec((tile, width), lambda i: (i, 0)),
+            whole(pairs.shape),
+            pl.BlockSpec((dec_slot.shape[0], tile), lambda i: (0, i)),
+            whole(table.shape),
+            pl.BlockSpec((tile, model), lambda i: (i, 0)),
+            whole(w_o_dec.shape),
+        ],
+        out_specs=pl.BlockSpec((tile, model), lambda i: (i, 0)),
+        scratch_shapes=[pltpu.VMEM((width, pairs.shape[0]), BF16), pltpu.VMEM((width, tile), BF16)],
+    )(queries, pairs, dec_slot, table, grid, w_o_dec)
+
+
+def by_kernels(grid, latent_in, grid_gain, node_gain, dec_gain, w_q_enc, w_kv_enc, w_o_enc,
+               w_q_dec, w_kv_dec, w_o_dec, enc_need, enc_slot, enc_count, dec_need, dec_slot):
+    latent_out, pairs, queries = encode(
+        grid, latent_in, grid_gain, node_gain, dec_gain, w_q_enc, w_kv_enc, w_o_enc, w_q_dec, w_kv_dec,
+        enc_need, enc_slot, enc_count)
+    grid_out = decode(queries, pairs, dec_slot, dec_need, grid, w_o_dec, latent_in.shape[0])
+    return (latent_out, grid_out)
+
+
+def chosen_form(*args):
+    grid, latent_in, enc_need, dec_slot = args[0], args[1], args[11], args[15]
+    peers = lax.axis_size("dom")
+    cap = enc_need.shape[1] // peers
+    small = latent_in.shape[0] * peers <= 256
+    fits = cap % 32 == 0 and HEADS * latent_in.shape[0] == 128 and grid.shape[0] % 256 == 0
+    if small and fits and 8 % dec_slot.shape[0] == 0:
+        return by_kernels(*args)
+    return on_device(*args)
+
+
 def solution(mesh):
     both, rep = P(("groups", "dom"), None), P()
     return jax.shard_map(
-        on_device,
+        chosen_form,
         mesh=mesh,
         in_specs=(both, both, *([rep] * 9), P("dom", None), P(None, "dom"), P("dom"), P("dom", None), P(None, "dom")),
         out_specs=(both, both),

time: 103 us -> 59 us (0.57)
  the two profiles are of different devices: /device:TPU:0 before, /device:TPU:31 now
where the time goes in v2:
time: 59 us; the launch traced here: 58.7 us
  Pallas kernels  56.1 us (95%)
  local copies, waits for them, and re-layouts  2 us (3%)
  between operations  0.65 us (1%)
    pallas_call x1, Pallas kernels, encode(): pl.pallas_call(functools.partial(encoder_kernel, peers), name='encode', o...  41.5 us
    pallas_call x1, Pallas kernels, decode(): pl.pallas_call(functools.partial(decoder_kernel, dec_need.shape[1] // pee...  14.6 us
    unnamed x4, local copies, waits for them, and re-layouts  2 us

profile of v2, /device:TPU:31, one launch (start us, length us, event | category | flops | bytes accessed | tf_op | source)
XLA Modules:
  0.0 58.7 jit_solution(15392098922727732569)
XLA Ops:
  0.6 1.4 %copy.18.slot_ref = s32[32,16]{1,0:T(8,128)} copy(s32[32,16]{0,1:T(8,128)} %param.28) | data formatting | bytes 4096 | tf_op args[12]
  2.0 41.5 %encode.1 = (bf16[16,1024]{1,0:T(8,128)(2,1)}, bf16[256,1024]{1,0:T(8,128)(2,1)}, bf16[1024,512]{1,0:T(8,128)(2,1)}) custom-call(bf16[1024,1024]{1,0:T(8,128)(2,1)} %grid_ref.1, bf16[16,1024]{1,0:T(8,128)(2,1)} %latent_ref.1, f32[1,1024]{1,0:T(1,128)} %bitcast.6, f32[1,1024]{1,0:T(1,128)} %bitcast.7, f32[1,1024]{1,0:T(1,128)} %bitcast.8, ...), custom_call_target="tpu_custom_call" | custom-call | tf_op jit(solution)/shard_map/encode/pallas_call | solution.py:280
  43.5 0.0 copy-start
  43.5 14.6 %decode.1 = bf16[1024,1024]{1,0:T(8,128)(2,1)} custom-call(bf16[1024,512]{1,0:T(8,128)(2,1)} %get-tuple-element.6.query_ref, bf16[256,1024]{1,0:T(8,128)(2,1)} %get-tuple-element.7.pairs_ref, s32[4,1024]{1,0:T(4,128)} %slot_ref.2, s32[32,128]{1,0:T(8,128)} %bitcast.5, bf16[1024,1024]{1,0:T(8,128)(2,1)} %grid_ref.1, bf16[512,1024]{1,0:T(8,128)(2,1)} %wo_ref.1), custom_call_target="tpu_custom_call" | custom-call | tf_op jit(solution)/shard_map/decode/pallas_call | solution.py:373
  58.1 0.0 copy-done
  58.1 0.6 %copy.20 = bf16[16,1024]{1,0:T(8,128)(2,1)} copy(bf16[16,1024]{1,0:T(8,128)(2,1)S(1)} %copy-done) | data formatting | bytes 65536
Async XLA Ops:
  43.5 14.6 %copy-start = (bf16[16,1024]{1,0:T(8,128)(2,1)S(1)}, bf16[16,1024]{1,0:T(8,128)(2,1)}, u32[]{:S(2)}) copy-start(bf16[16,1024]{1,0:T(8,128)(2,1)} %get-tuple-element.10) | copy-start | bytes 98308

commit v3 on v2

--- a/solution.py
+++ b/solution.py
@@ -92,14 +92,18 @@
     need_ref, slot_ref, count_ref,
     latent_out, pairs_out, queries_out,
     grid_v, wq_v, wkv_v, wo_v, wqd_v, wkvd_v, normed, rows, query_mine, edges_mine,
-    need_all, query_all, edges_all, mix_send, stat_send, mix_all, stat_all, pairs_all,
+    need_all, query_all, edges_all, times_all, mix_send, stat_send, mix_all, stat_all, pairs_all,
     load_sem, send_sem, recv_sem,
 ):
     me = lax.axis_index("dom")
     nodes, model = latent_ref.shape
     width = wq_v.shape[1]
     head = width // HEADS
-    cap = edges_all.shape[1]
+    cap = need_ref.shape[1] // peers
+    group = 128 // cap
+    chips = peers // 2
+    side = lax.rem(me, 2)
+    partner = me + 1 - 2 * side
     points = grid_v.shape[0]
     lanes = HEADS * nodes
 
@@ -118,11 +122,11 @@
             barrier, inc=1, device_id={"dom": lax.rem(me + step, peers)}, device_id_type=pl.DeviceIdType.MESH
         )
 
-    def message(kind, source, target, to, slot):
+    def message(kind, source, target, to, slot, way=None):
         return pltpu.make_async_remote_copy(
             src_ref=source,
             dst_ref=target,
-            send_sem=send_sem.at[kind, to],
+            send_sem=send_sem.at[kind, to if way is None else way],
             recv_sem=recv_sem.at[kind, slot],
             device_id={"dom": to},
             device_id_type=pl.DeviceIdType.MESH,
@@ -134,8 +138,14 @@
     def query_to(to, slot):
         return message(1, query_mine, query_all.at[slot], to, slot)
 
+    def query_on(owner, slot):
+        return message(6, query_all.at[owner], query_all.at[slot], partner, slot, owner)
+
+    def pairs_on(owner, slot):
+        return message(7, pairs_all.at[owner], pairs_all.at[slot], partner, slot, owner)
+
     def edges_to(to, slot):
-        return message(2, edges_mine.at[to], edges_all.at[slot], to, slot)
+        return message(2, edges_mine.at[to // group], edges_all.at[slot], to, slot)
 
     def mix_to(to, slot):
         return message(3, mix_send.at[to], mix_all.at[slot], to, slot)
@@ -152,6 +162,13 @@
             return carry
 
         lax.fori_loop(1, peers, body, 0)
+
+    def each_chip(act):
+        def body(step, carry):
+            act(lax.rem(me + 2 * step, peers))
+            return carry
+
+        lax.fori_loop(1, chips, body, 0)
 
     pl.semaphore_wait(barrier, peers - 1)
     each_peer(lambda to: need_to(to, me).start())
@@ -163,20 +180,19 @@
     ).astype(BF16)
     query_mine[...] = queries
     query_all[me] = queries
-    each_peer(lambda to: query_to(to, me).start())
-
-    edge_total = slot_ref.shape[0]
-    slots = jnp.where(iota(slot_ref.shape, 0) < count_ref[...], slot_ref[...], -1).astype(F32)
-    turn = (iota((edge_total, edge_total), 0) == iota((edge_total, edge_total), 1)).astype(F32)
-    by_node = lax.dot_general(slots, turn, TN, precision=HIGH, preferred_element_type=F32)
-    entry = iota((nodes, peers * cap), 1).astype(F32)
+    query_to(partner, me).start()
+    each_chip(lambda to: query_to(to, me).start())
+
+    edge_total = slot_ref.shape[1]
+    slots = jnp.where(iota(slot_ref.shape, 1) < count_ref[...], slot_ref[...], -1)
+    entry = iota((nodes, peers * cap), 1)
     tally = jnp.zeros((nodes, peers * cap), F32)
     for j in range(edge_total):
-        tally = tally + jnp.where(by_node[:, j : j + 1] == entry, 1.0, 0.0)
-    spread_out = (iota((nodes, lanes), 0) == lax.rem(iota((nodes, lanes), 1), nodes)).astype(BF16)
-    tally = lax.dot_general(tally.astype(BF16), spread_out, TN, preferred_element_type=F32)
-    edges_mine[...] = tally.astype(BF16).reshape(peers, cap, lanes)
-    edges_all[me] = edges_mine[me]
+        tally = tally + jnp.where(slots[:, j : j + 1] == entry, 1.0, 0.0)
+    tally = tally.astype(BF16)
+    for part in range(peers // group):
+        edges_mine[part] = tally[:, part * 128 : (part + 1) * 128]
+    edges_all[me] = edges_mine[me // group]
     each_peer(lambda to: edges_to(to, me).start())
 
     loads[1].wait()
@@ -199,6 +215,23 @@
     loads[2].wait()
     rows[...] = jnp.dot(chosen, wkv_v[...], preferred_element_type=F32).astype(BF16)
 
+    def pass_query(peer):
+        query_to(peer, peer).wait_recv()
+        query_on(peer, peer).start()
+
+    each_chip(pass_query)
+    each_peer(lambda peer: edges_to(peer, peer).wait_recv())
+    mine = iota((cap, 128), 1) == lax.rem(me, group) * cap + iota((cap, 128), 0)
+    entries = lax.dot_general(
+        mine.astype(BF16), edges_all[...].reshape(peers * nodes, 128), NT, preferred_element_type=F32
+    ).astype(BF16)
+    fan = iota((peers * nodes, peers * lanes), 0)
+    fan_lane = iota((peers * nodes, peers * lanes), 1)
+    fan = fan == (fan_lane // lanes) * nodes + lax.rem(fan_lane, nodes)
+    entries = jnp.dot(entries, jnp.where(fan, 1.0, 0.0).astype(BF16), preferred_element_type=F32)
+    for peer in range(peers):
+        times_all[peer] = entries[:, peer * lanes : (peer + 1) * lanes]
+
     own_head = iota((lanes, width), 0) // nodes == iota((lanes, width), 1) // head
 
     def window(w):
@@ -206,7 +239,7 @@
         spread_query = jnp.where(own_head, spread_query, jnp.zeros_like(spread_query))
         here = pl.ds(pl.multiple_of(w * cap, cap), cap)
         scores = lax.dot_general(rows[here, :width], spread_query, NT, preferred_element_type=F32)
-        times = edges_all[w].astype(F32)
+        times = times_all[w]
         scores = jnp.where(times > 0, scores * (1.0 / math.sqrt(head)), -1e30)
         highest = jnp.max(scores, axis=0, keepdims=True)
         raised = jnp.exp(scores - highest) * times
@@ -215,17 +248,27 @@
         mixed = jnp.where(own_head, mixed, 0.0).reshape(HEADS, nodes, width)
         return jnp.sum(mixed, axis=0).astype(BF16), highest, total
 
-    def serve(peer):
-        query_to(peer, peer).wait_recv()
-        edges_to(peer, peer).wait_recv()
-        mixed, highest, total = window(peer)
-        mix_send[peer] = mixed
-        stat_send[peer, 0:1, :] = highest
-        stat_send[peer, 1:2, :] = total
+    def serve(windows):
+        for peer, answer in [(peer, window(peer)) for peer in windows]:
+            mix_send[peer] = answer[0]
+            stat_send[peer, 0:1, :] = answer[1]
+            stat_send[peer, 1:2, :] = answer[2]
+
+    def reply(peer):
         mix_to(peer, me).start()
         stat_to(peer, me).start()
 
-    each_peer(serve)
+    serve([lax.rem(me + 2 * step, peers) for step in range(1, chips)])
+    each_chip(reply)
+    query_to(partner, partner).wait_recv()
+
+    def take_passed(peer):
+        owner = peer + 1 - 2 * side
+        query_on(owner, owner).wait_recv()
+
+    each_chip(take_passed)
+    serve([lax.rem(partner + 2 * step, peers) for step in range(chips)])
+    lax.fori_loop(0, chips, lambda step, carry: (reply(lax.rem(partner + 2 * step, peers)), carry)[1], 0)
     mixed, highest, total = window(me)
     mix_all[me] = mixed
     stat_all[me, 0:1, :] = highest
@@ -256,15 +299,37 @@
     loads[5].wait()
     pairs = jnp.dot(norm_into(fresh, dgain_ref[...]), wkvd_v[...], preferred_element_type=F32).astype(BF16)
     pairs_all[me] = pairs
-    each_peer(lambda to: pairs_to(to, me).start())
-    each_peer(lambda peer: pairs_to(peer, peer).wait_recv())
+    each_chip(lambda to: pairs_to(to, me).start())
+    pairs_to(partner, me).start()
+
+    def pass_pairs(peer):
+        pairs_to(peer, peer).wait_recv()
+        pairs_on(peer, peer).start()
+
+    each_chip(pass_pairs)
+    pairs_to(partner, partner).wait_recv()
+
+    def take_pairs(peer):
+        owner = peer + 1 - 2 * side
+        pairs_on(owner, owner).wait_recv()
+
+    each_chip(take_pairs)
     pairs_out[...] = pairs_all[...].reshape(peers * nodes, model)
 
     def drain(to):
-        for outgoing in (need_to, query_to, edges_to, mix_to, stat_to, pairs_to):
+        for outgoing in (need_to, edges_to, mix_to, stat_to):
             outgoing(to, me).wait_send()
 
+    def drain_chip(to):
+        query_to(to, me).wait_send()
+        pairs_to(to, me).wait_send()
+        query_on(to, to).wait_send()
+        pairs_on(to, to).wait_send()
+
     each_peer(drain)
+    each_chip(drain_chip)
+    query_to(partner, me).wait_send()
+    pairs_to(partner, me).wait_send()
 
 
 def encode(grid, latent_in, grid_gain, node_gain, dec_gain, w_q_enc, w_kv_enc, w_o_enc, w_q_dec, w_kv_dec,
@@ -297,34 +362,43 @@
             pltpu.VMEM(grid.shape, BF16),
             pltpu.VMEM((entries, 2 * width), BF16),
             pltpu.VMEM((nodes, width), BF16),
-            pltpu.VMEM((peers, cap, HEADS * nodes), BF16),
+            pltpu.VMEM((entries // 128, nodes, 128), BF16),
             pltpu.VMEM((peers, 1, entries), jnp.int32),
             pltpu.VMEM((peers, nodes, width), BF16),
-            pltpu.VMEM((peers, cap, HEADS * nodes), BF16),
+            pltpu.VMEM((peers, nodes, 128), BF16),
+            pltpu.VMEM((peers, cap, HEADS * nodes), F32),
             pltpu.VMEM((peers, nodes, width), BF16),
             pltpu.VMEM((peers, 2, HEADS * nodes), F32),
             pltpu.VMEM((peers, nodes, width), BF16),
             pltpu.VMEM((peers, 2, HEADS * nodes), F32),
             pltpu.VMEM((peers, nodes, 2 * width), BF16),
             pltpu.SemaphoreType.DMA((6,)),
-            pltpu.SemaphoreType.DMA((6, peers)),
-            pltpu.SemaphoreType.DMA((6, peers)),
+            pltpu.SemaphoreType.DMA((8, peers)),
+            pltpu.SemaphoreType.DMA((8, peers)),
         ],
         compiler_params=pltpu.CompilerParams(
             collective_id=0, has_side_effects=True, vmem_limit_bytes=60 * 1024 * 1024
         ),
     )(grid, latent_in, grid_gain[None], node_gain[None], dec_gain[None], w_q_enc, w_kv_enc, w_o_enc, w_q_dec,
-      w_kv_dec, enc_need, enc_slot, enc_count[None])
-
-
-def decoder_kernel(cap, nodes, query_ref, pairs_ref, slot_ref, table_ref, grid_ref, wo_ref, out_ref, turned, mixed):
+      w_kv_dec, enc_need, enc_slot.T, enc_count[:, None])
+
+
+def decoder_kernel(cap, nodes, query_ref, pairs_ref, slot_ref, table_ref, grid_ref, wo_ref, latent_ref, out_ref, latent_out, keys_of, turned, mixed):
     tile, width = query_ref.shape
     head = width // HEADS
     keys = pairs_ref.shape[0]
+    quad = 4
 
     @pl.when(pl.program_id(0) == 0)
     def _():
         turned[...] = pairs_ref[:, width:].astype(F32).T.astype(BF16)
+        latent_out[...] = latent_ref[...]
+        lane_head = iota((keys, quad * head), 1) // head
+        for h in range(HEADS):
+            some = pairs_ref[:, (h // quad) * quad * head : (h // quad + 1) * quad * head] * (1.0 / math.sqrt(head))
+            keys_of[h // quad, (h % quad) * keys : (h % quad + 1) * keys, :] = jnp.where(
+                lane_head == h % quad, some, jnp.zeros_like(some)
+            )
 
     slots = slot_ref[...]
     edge_total = slots.shape[0]
@@ -345,14 +419,11 @@
     for j in range(edge_total):
         times = times + jnp.where(node[j : j + 1, :] == name, 1.0, 0.0)
     bias = jnp.where(times > 0, jnp.log(jnp.maximum(times, 1.0)), -1e30)
-    lanes_of = iota((keys, 2 * head), 1) // head
-    for pair in range(HEADS // 2):
-        at = slice(pair * 2 * head, (pair + 1) * 2 * head)
-        query = query_ref[:, at]
-        key = pairs_ref[:, at] * (1.0 / math.sqrt(head))
-        for side in range(2):
-            h = pair * 2 + side
-            own = jnp.where(lanes_of == side, key, jnp.zeros_like(key))
+    for four in range(HEADS // quad):
+        query = query_ref[:, four * quad * head : (four + 1) * quad * head]
+        for side in range(quad):
+            h = four * quad + side
+            own = keys_of[four, side * keys : (side + 1) * keys, :]
             scores = lax.dot_general(own, query, NT, preferred_element_type=F32) + bias
             highest = jnp.max(scores, axis=0, keepdims=True)
             raised = jnp.exp(scores - highest)
@@ -363,18 +434,22 @@
     out_ref[...] = (grid_ref[...].astype(F32) + update).astype(BF16)
 
 
-def decode(queries, pairs, dec_slot, dec_need, grid, w_o_dec, nodes):
+def decode(queries, pairs, dec_slot, dec_need, grid, w_o_dec, latent_out):
     peers = lax.axis_size("dom")
     points, model = grid.shape
     width = queries.shape[1]
-    tile = 256
+    nodes = latent_out.shape[0]
+    tile = 512
     table = dec_need.reshape(-1, 128)
     whole = lambda shape: pl.BlockSpec(shape, lambda i: (0, 0))
     return pl.pallas_call(
         functools.partial(decoder_kernel, dec_need.shape[1] // peers, nodes),
         name="decode",
         grid=(points // tile,),
-        out_shape=jax.ShapeDtypeStruct(grid.shape, BF16),
+        out_shape=(
+            jax.ShapeDtypeStruct(grid.shape, BF16),
+            jax.ShapeDtypeStruct(latent_out.shape, BF16),
+        ),
         in_specs=[
             pl.BlockSpec((tile, width), lambda i: (i, 0)),
             whole(pairs.shape),
@@ -382,10 +457,11 @@
             whole(table.shape),
             pl.BlockSpec((tile, model), lambda i: (i, 0)),
             whole(w_o_dec.shape),
+            whole(latent_out.shape),
         ],
-        out_specs=pl.BlockSpec((tile, model), lambda i: (i, 0)),
-        scratch_shapes=[pltpu.VMEM((width, pairs.shape[0]), BF16), pltpu.VMEM((width, tile), BF16)],
-    )(queries, pairs, dec_slot, table, grid, w_o_dec)
+        out_specs=(pl.BlockSpec((tile, model), lambda i: (i, 0)), whole(latent_out.shape)),
+        scratch_shapes=[pltpu.VMEM((2, 4 * pairs.shape[0], width // 2), BF16), pltpu.VMEM((width, pairs.shape[0]), BF16), pltpu.VMEM((width, tile), BF16)],
+    )(queries, pairs, dec_slot, table, grid, w_o_dec, latent_out)
 
 
 def by_kernels(grid, latent_in, grid_gain, node_gain, dec_gain, w_q_enc, w_kv_enc, w_o_enc,
@@ -393,7 +469,7 @@
     latent_out, pairs, queries = encode(
         grid, latent_in, grid_gain, node_gain, dec_gain, w_q_enc, w_kv_enc, w_o_enc, w_q_dec, w_kv_dec,
         enc_need, enc_slot, enc_count)
-    grid_out = decode(queries, pairs, dec_slot, dec_need, grid, w_o_dec, latent_in.shape[0])
+    grid_out, latent_out = decode(queries, pairs, dec_slot, dec_need, grid, w_o_dec, latent_out)
     return (latent_out, grid_out)
 
 
@@ -402,7 +478,7 @@
     peers = lax.axis_size("dom")
     cap = enc_need.shape[1] // peers
     small = latent_in.shape[0] * peers <= 256
-    fits = cap % 32 == 0 and HEADS * latent_in.shape[0] == 128 and grid.shape[0] % 256 == 0
+    fits = peers % 2 == 0 and 128 % cap == 0 and cap % 32 == 0 and HEADS * latent_in.shape[0] == 128 and grid.shape[0] % 512 == 0
     if small and fits and 8 % dec_slot.shape[0] == 0:
         return by_kernels(*args)
     return on_device(*args)

time: 59 us -> 48.6 us (0.82)
  the two profiles are of different devices: /device:TPU:31 before, /device:TPU:0 now
where the time goes in v3:
time: 48.6 us; the launch traced here: 48.3 us
  Pallas kernels  46.3 us (95%)
  local copies, waits for them, and re-layouts  1.33 us (3%)
  between operations  0.64 us (1%)
    pallas_call x1, Pallas kernels, encode(): pl.pallas_call(functools.partial(encoder_kernel, peers), name='encode', o...  34.4 us
    pallas_call x1, Pallas kernels, decode(): pl.pallas_call(functools.partial(decoder_kernel, dec_need.shape[1] // pee...  11.9 us
    broadcast_in_dim x1, local copies, waits for them, and re-layouts, encode(): enc_count[:, None]  1.33 us

profile of v3, /device:TPU:0, one launch (start us, length us, event | category | flops | bytes accessed | tf_op | source)
XLA Modules:
  0.0 48.3 jit_solution(3100678084598859395)
XLA Ops:
  0.6 1.3 %copy.18.count_ref = s32[16,1]{1,0:T(8,128)} copy(s32[16,1]{0,1:T(1,128)} %bitcast.11) | data formatting | bytes 128 | tf_op jit(solution)/shard_map/broadcast_in_dim | solution.py:383
  2.0 34.4 %encode.1 = (bf16[16,1024]{1,0:T(8,128)(2,1)}, bf16[256,1024]{1,0:T(8,128)(2,1)}, bf16[1024,512]{1,0:T(8,128)(2,1)}) custom-call(bf16[1024,1024]{1,0:T(8,128)(2,1)} %grid_ref.1, bf16[16,1024]{1,0:T(8,128)(2,1)} %latent_ref.1, f32[1,1024]{1,0:T(1,128)} %bitcast.8, f32[1,1024]{1,0:T(1,128)} %bitcast.9, f32[1,1024]{1,0:T(1,128)} %bitcast.10, ...), custom_call_target="tpu_custom_call" | custom-call | tf_op jit(solution)/shard_map/encode/pallas_call | solution.py:345
  36.3 11.9 %decode.1 = (bf16[1024,1024]{1,0:T(8,128)(2,1)}, bf16[16,1024]{1,0:T(8,128)(2,1)}) custom-call(bf16[1024,512]{1,0:T(8,128)(2,1)} %get-tuple-element.7.query_ref, bf16[256,1024]{1,0:T(8,128)(2,1)} %get-tuple-element.8.pairs_ref, s32[4,1024]{1,0:T(4,128)} %slot_ref.1, s32[32,128]{1,0:T(8,128)} %bitcast.6, bf16[1024,1024]{1,0:T(8,128)(2,1)} %grid_ref.1, ...), custom_call_target="tpu_custom_call" | custom-call | tf_op jit(solution)/shard_map/decode/pallas_call | solution.py:445

commit v4 on v3

--- a/solution.py
+++ b/solution.py
@@ -89,8 +89,8 @@
 
 def encoder_kernel(
     peers, grid_hbm, latent_ref, ggain_ref, ngain_ref, dgain_ref, wq_hbm, wkv_hbm, wo_hbm, wqd_hbm, wkvd_hbm,
-    need_ref, slot_ref, count_ref,
-    latent_out, pairs_out, queries_out,
+    need_ref, slot_ref, count_ref, dslot_ref, table_ref,
+    latent_out, pairs_out, queries_out, bias_out,
     grid_v, wq_v, wkv_v, wo_v, wqd_v, wkvd_v, normed, rows, query_mine, edges_mine,
     need_all, query_all, edges_all, times_all, mix_send, stat_send, mix_all, stat_all, pairs_all,
     load_sem, send_sem, recv_sem,
@@ -170,21 +170,10 @@
 
         lax.fori_loop(1, chips, body, 0)
 
-    pl.semaphore_wait(barrier, peers - 1)
-    each_peer(lambda to: need_to(to, me).start())
-    need_all[me] = need_ref[...]
-
-    loads[0].wait()
-    queries = jnp.dot(
-        norm_into(latent_ref[...], ngain_ref[...]), wq_v[...], preferred_element_type=F32
-    ).astype(BF16)
-    query_mine[...] = queries
-    query_all[me] = queries
-    query_to(partner, me).start()
-    each_chip(lambda to: query_to(to, me).start())
-
     edge_total = slot_ref.shape[1]
-    slots = jnp.where(iota(slot_ref.shape, 1) < count_ref[...], slot_ref[...], -1)
+    own = iota((nodes, nodes), 0) == iota((nodes, nodes), 1)
+    counts = jnp.sum(jnp.where(own, count_ref[...].astype(F32), 0.0), axis=1, keepdims=True)
+    slots = jnp.where(iota(slot_ref.shape, 1).astype(F32) < counts, slot_ref[...], -1)
     entry = iota((nodes, peers * cap), 1)
     tally = jnp.zeros((nodes, peers * cap), F32)
     for j in range(edge_total):
@@ -193,6 +182,18 @@
     for part in range(peers // group):
         edges_mine[part] = tally[:, part * 128 : (part + 1) * 128]
     edges_all[me] = edges_mine[me // group]
+    loads[0].wait()
+    queries = jnp.dot(
+        norm_into(latent_ref[...], ngain_ref[...]), wq_v[...], preferred_element_type=F32
+    ).astype(BF16)
+    query_mine[...] = queries
+    query_all[me] = queries
+    need_all[me] = need_ref[...]
+
+    pl.semaphore_wait(barrier, peers - 1)
+    each_peer(lambda to: need_to(to, me).start())
+    query_to(partner, me).start()
+    each_chip(lambda to: query_to(to, me).start())
     each_peer(lambda to: edges_to(to, me).start())
 
     loads[1].wait()
@@ -212,14 +213,15 @@
     wanted = wanted.reshape(peers * cap, 1)
     pick = jnp.where(wanted == iota((peers * cap, points), 1), 1.0, 0.0).astype(BF16)
     chosen = jnp.dot(pick, normed[...], preferred_element_type=F32).astype(BF16)
-    loads[2].wait()
-    rows[...] = jnp.dot(chosen, wkv_v[...], preferred_element_type=F32).astype(BF16)
-
     def pass_query(peer):
         query_to(peer, peer).wait_recv()
         query_on(peer, peer).start()
 
     each_chip(pass_query)
+
+    loads[2].wait()
+    rows[...] = jnp.dot(chosen, wkv_v[...], preferred_element_type=F32).astype(BF16)
+
     each_peer(lambda peer: edges_to(peer, peer).wait_recv())
     mine = iota((cap, 128), 1) == lax.rem(me, group) * cap + iota((cap, 128), 0)
     entries = lax.dot_general(
@@ -276,6 +278,28 @@
 
     loads[3].wait()
     queries_out[...] = jnp.dot(normed[...], wqd_v[...], preferred_element_type=F32).astype(BF16)
+
+    keys = peers * nodes
+    dec_cap = table_ref.shape[0] * 128 // peers
+    slots = dslot_ref[...]
+    edge_total = slots.shape[0]
+    slots = jnp.concatenate([slots] * (8 // edge_total), axis=0)
+    columns = []
+    for part in range(points // 128):
+        piece = slots[:, part * 128 : (part + 1) * 128]
+        high = piece // 128
+        low = lax.rem(piece, 128)
+        need = jnp.zeros_like(piece)
+        for line in range(table_ref.shape[0]):
+            entry = jnp.broadcast_to(table_ref[line : line + 1, :], piece.shape)
+            need = jnp.where(high == line, jnp.take_along_axis(entry, low, axis=1), need)
+        columns.append((piece // dec_cap) * nodes + need)
+    node = jnp.concatenate(columns, axis=1)
+    name = iota((keys, points), 0)
+    times = jnp.zeros((keys, points), F32)
+    for j in range(edge_total):
+        times = times + jnp.where(node[j : j + 1, :] == name, 1.0, 0.0)
+    bias_out[...] = jnp.where(times > 0, jnp.log(jnp.maximum(times, 1.0)), -1e30)
 
     def take_mix(peer):
         mix_to(peer, peer).wait_recv()
@@ -333,7 +357,7 @@
 
 
 def encode(grid, latent_in, grid_gain, node_gain, dec_gain, w_q_enc, w_kv_enc, w_o_enc, w_q_dec, w_kv_dec,
-           enc_need, enc_slot, enc_count):
+           enc_need, enc_slot, enc_count, dec_slot, dec_need):
     peers = lax.axis_size("dom")
     nodes, model = latent_in.shape
     width = w_q_enc.shape[1]
@@ -349,9 +373,10 @@
             jax.ShapeDtypeStruct((nodes, model), BF16),
             jax.ShapeDtypeStruct((peers * nodes, 2 * width), BF16),
             jax.ShapeDtypeStruct((points, width), BF16),
+            jax.ShapeDtypeStruct((peers * nodes, points), F32),
         ),
-        in_specs=[far, vmem, vmem, vmem, vmem, far, far, far, far, far, vmem, vmem, vmem],
-        out_specs=(vmem, vmem, vmem),
+        in_specs=[far, vmem, vmem, vmem, vmem, far, far, far, far, far, vmem, vmem, vmem, vmem, vmem],
+        out_specs=(vmem, vmem, vmem, vmem),
         scratch_shapes=[
             pltpu.VMEM(grid.shape, BF16),
             pltpu.VMEM(w_q_enc.shape, BF16),
@@ -380,10 +405,10 @@
             collective_id=0, has_side_effects=True, vmem_limit_bytes=60 * 1024 * 1024
         ),
     )(grid, latent_in, grid_gain[None], node_gain[None], dec_gain[None], w_q_enc, w_kv_enc, w_o_enc, w_q_dec,
-      w_kv_dec, enc_need, enc_slot.T, enc_count[:, None])
-
-
-def decoder_kernel(cap, nodes, query_ref, pairs_ref, slot_ref, table_ref, grid_ref, wo_ref, latent_ref, out_ref, latent_out, keys_of, turned, mixed):
+      w_kv_dec, enc_need, enc_slot.T, enc_count[None], dec_slot, dec_need.reshape(-1, 128))
+
+
+def decoder_kernel(query_ref, pairs_ref, bias_ref, grid_ref, wo_ref, latent_ref, out_ref, latent_out, keys_of, turned, mixed):
     tile, width = query_ref.shape
     head = width // HEADS
     keys = pairs_ref.shape[0]
@@ -400,31 +425,12 @@
                 lane_head == h % quad, some, jnp.zeros_like(some)
             )
 
-    slots = slot_ref[...]
-    edge_total = slots.shape[0]
-    slots = jnp.concatenate([slots] * (8 // edge_total), axis=0)
-    columns = []
-    for part in range(tile // 128):
-        piece = slots[:, part * 128 : (part + 1) * 128]
-        high = piece // 128
-        low = lax.rem(piece, 128)
-        need = jnp.zeros_like(piece)
-        for line in range(table_ref.shape[0]):
-            entry = jnp.broadcast_to(table_ref[line : line + 1, :], piece.shape)
-            need = jnp.where(high == line, jnp.take_along_axis(entry, low, axis=1), need)
-        columns.append((piece // cap) * nodes + need)
-    node = jnp.concatenate(columns, axis=1)
-    name = iota((keys, tile), 0)
-    times = jnp.zeros((keys, tile), F32)
-    for j in range(edge_total):
-        times = times + jnp.where(node[j : j + 1, :] == name, 1.0, 0.0)
-    bias = jnp.where(times > 0, jnp.log(jnp.maximum(times, 1.0)), -1e30)
     for four in range(HEADS // quad):
         query = query_ref[:, four * quad * head : (four + 1) * quad * head]
         for side in range(quad):
             h = four * quad + side
             own = keys_of[four, side * keys : (side + 1) * keys, :]
-            scores = lax.dot_general(own, query, NT, preferred_element_type=F32) + bias
+            scores = lax.dot_general(own, query, NT, preferred_element_type=F32) + bias_ref[...]
             highest = jnp.max(scores, axis=0, keepdims=True)
             raised = jnp.exp(scores - highest)
             total = jnp.sum(raised, axis=0, keepdims=True)
@@ -434,16 +440,13 @@
     out_ref[...] = (grid_ref[...].astype(F32) + update).astype(BF16)
 
 
-def decode(queries, pairs, dec_slot, dec_need, grid, w_o_dec, latent_out):
-    peers = lax.axis_size("dom")
+def decode(queries, pairs, bias, grid, w_o_dec, latent_out):
     points, model = grid.shape
     width = queries.shape[1]
-    nodes = latent_out.shape[0]
-    tile = 512
-    table = dec_need.reshape(-1, 128)
+    tile = 1024
     whole = lambda shape: pl.BlockSpec(shape, lambda i: (0, 0))
     return pl.pallas_call(
-        functools.partial(decoder_kernel, dec_need.shape[1] // peers, nodes),
+        decoder_kernel,
         name="decode",
         grid=(points // tile,),
         out_shape=(
@@ -453,23 +456,22 @@
         in_specs=[
             pl.BlockSpec((tile, width), lambda i: (i, 0)),
             whole(pairs.shape),
-            pl.BlockSpec((dec_slot.shape[0], tile), lambda i: (0, i)),
-            whole(table.shape),
+            pl.BlockSpec((pairs.shape[0], tile), lambda i: (0, i)),
             pl.BlockSpec((tile, model), lambda i: (i, 0)),
             whole(w_o_dec.shape),
             whole(latent_out.shape),
         ],
         out_specs=(pl.BlockSpec((tile, model), lambda i: (i, 0)), whole(latent_out.shape)),
         scratch_shapes=[pltpu.VMEM((2, 4 * pairs.shape[0], width // 2), BF16), pltpu.VMEM((width, pairs.shape[0]), BF16), pltpu.VMEM((width, tile), BF16)],
-    )(queries, pairs, dec_slot, table, grid, w_o_dec, latent_out)
+    )(queries, pairs, bias, grid, w_o_dec, latent_out)
 
 
 def by_kernels(grid, latent_in, grid_gain, node_gain, dec_gain, w_q_enc, w_kv_enc, w_o_enc,
                w_q_dec, w_kv_dec, w_o_dec, enc_need, enc_slot, enc_count, dec_need, dec_slot):
-    latent_out, pairs, queries = encode(
+    latent_out, pairs, queries, bias = encode(
         grid, latent_in, grid_gain, node_gain, dec_gain, w_q_enc, w_kv_enc, w_o_enc, w_q_dec, w_kv_dec,
-        enc_need, enc_slot, enc_count)
-    grid_out, latent_out = decode(queries, pairs, dec_slot, dec_need, grid, w_o_dec, latent_out)
+        enc_need, enc_slot, enc_count, dec_slot, dec_need)
+    grid_out, latent_out = decode(queries, pairs, bias, grid, w_o_dec, latent_out)
     return (latent_out, grid_out)
 
 
@@ -478,7 +480,7 @@
     peers = lax.axis_size("dom")
     cap = enc_need.shape[1] // peers
     small = latent_in.shape[0] * peers <= 256
-    fits = peers % 2 == 0 and 128 % cap == 0 and cap % 32 == 0 and HEADS * latent_in.shape[0] == 128 and grid.shape[0] % 512 == 0
+    fits = peers % 2 == 0 and 128 % cap == 0 and cap % 32 == 0 and HEADS * latent_in.shape[0] == 128 and grid.shape[0] % 1024 == 0
     if small and fits and 8 % dec_slot.shape[0] == 0:
         return by_kernels(*args)
     return on_device(*args)

time: 48.6 us -> 45.8 us (0.942)
  Pallas kernels: 46.3 us -> 44.7 us
  local copies, waits for them, and re-layouts: 1.33 us -> 0 us
    pallas_call x1, Pallas kernels: 11.9 us -> 9.55 us  [decode(): pl.pallas_call(decoder_kernel, name='decode', grid=(points // tile,), out...]
    broadcast_in_dim x1 -> x0, local copies, waits for them, and re-layouts: 1.33 us -> none  [encode(): enc_count[:, None]]
    pallas_call x1, Pallas kernels: 34.4 us -> 35.1 us  [encode(): pl.pallas_call(functools.partial(encoder_kernel, peers), name='encode', o...]
where the time goes in v4:
time: 45.8 us; the launch traced here: 45.3 us
  Pallas kernels  44.7 us (98%)
  between operations  0.64 us (1%)
    pallas_call x1, Pallas kernels, encode(): pl.pallas_call(functools.partial(encoder_kernel, peers), name='encode', o...  35.1 us
    pallas_call x1, Pallas kernels, decode(): pl.pallas_call(decoder_kernel, name='decode', grid=(points // tile,), out...  9.55 us

profile of v4, /device:TPU:0, one launch (start us, length us, event | category | flops | bytes accessed | tf_op | source)
XLA Modules:
  0.0 45.3 jit_solution(4011757592689776260)
XLA Ops:
  0.6 35.1 %encode.1 = (bf16[16,1024]{1,0:T(8,128)(2,1)}, bf16[256,1024]{1,0:T(8,128)(2,1)}, bf16[1024,512]{1,0:T(8,128)(2,1)}, f32[256,1024]{1,0:T(8,128)}) custom-call(bf16[1024,1024]{1,0:T(8,128)(2,1)} %grid_ref.1, bf16[16,1024]{1,0:T(8,128)(2,1)} %latent_ref.1, f32[1,1024]{1,0:T(1,128)} %bitcast.8, f32[1,1024]{1,0:T(1,128)} %bitcast.9, f32[1,1024]{1,0:T(1,128)} %bitcast.10, ...), custom_call_target="tpu_custom_call" | custom-call | tf_op jit(solution)/shard_map/encode/pallas_call | solution.py:369
  35.8 9.6 %decode.1 = (bf16[1024,1024]{1,0:T(8,128)(2,1)}, bf16[16,1024]{1,0:T(8,128)(2,1)}) custom-call(bf16[1024,512]{1,0:T(8,128)(2,1)} %get-tuple-element.8.query_ref, bf16[256,1024]{1,0:T(8,128)(2,1)} %get-tuple-element.9.pairs_ref, f32[256,1024]{1,0:T(8,128)} %get-tuple-element.10.bias_ref, bf16[1024,1024]{1,0:T(8,128)(2,1)} %grid_ref.1, ...), custom_call_target="tpu_custom_call" | custom-call | tf_op jit(solution)/shard_map/decode/pallas_call | solution.py:448

commit v5 on v4

--- a/solution.py
+++ b/solution.py
@@ -90,10 +90,10 @@
 def encoder_kernel(
     peers, grid_hbm, latent_ref, ggain_ref, ngain_ref, dgain_ref, wq_hbm, wkv_hbm, wo_hbm, wqd_hbm, wkvd_hbm,
     need_ref, slot_ref, count_ref, dslot_ref, table_ref,
-    latent_out, pairs_out, queries_out, bias_out,
+    latent_out, pairs_out, queries_hbm, bias_hbm,
     grid_v, wq_v, wkv_v, wo_v, wqd_v, wkvd_v, normed, rows, query_mine, edges_mine,
     need_all, query_all, edges_all, times_all, mix_send, stat_send, mix_all, stat_all, pairs_all,
-    load_sem, send_sem, recv_sem,
+    queries_out, bias_out, load_sem, store_sem, send_sem, recv_sem,
 ):
     me = lax.axis_index("dom")
     nodes, model = latent_ref.shape
@@ -217,11 +217,11 @@
         query_to(peer, peer).wait_recv()
         query_on(peer, peer).start()
 
-    each_chip(pass_query)
 
     loads[2].wait()
     rows[...] = jnp.dot(chosen, wkv_v[...], preferred_element_type=F32).astype(BF16)
 
+    each_chip(pass_query)
     each_peer(lambda peer: edges_to(peer, peer).wait_recv())
     mine = iota((cap, 128), 1) == lax.rem(me, group) * cap + iota((cap, 128), 0)
     entries = lax.dot_general(
@@ -278,6 +278,8 @@
 
     loads[3].wait()
     queries_out[...] = jnp.dot(normed[...], wqd_v[...], preferred_element_type=F32).astype(BF16)
+    queries_store = pltpu.make_async_copy(queries_out, queries_hbm, store_sem.at[0])
+    queries_store.start()
 
     keys = peers * nodes
     dec_cap = table_ref.shape[0] * 128 // peers
@@ -300,6 +302,8 @@
     for j in range(edge_total):
         times = times + jnp.where(node[j : j + 1, :] == name, 1.0, 0.0)
     bias_out[...] = jnp.where(times > 0, jnp.log(jnp.maximum(times, 1.0)), -1e30)
+    bias_store = pltpu.make_async_copy(bias_out, bias_hbm, store_sem.at[1])
+    bias_store.start()
 
     def take_mix(peer):
         mix_to(peer, peer).wait_recv()
@@ -350,6 +354,8 @@
         query_on(to, to).wait_send()
         pairs_on(to, to).wait_send()
 
+    queries_store.wait()
+    bias_store.wait()
     each_peer(drain)
     each_chip(drain_chip)
     query_to(partner, me).wait_send()
@@ -376,7 +382,7 @@
             jax.ShapeDtypeStruct((peers * nodes, points), F32),
         ),
         in_specs=[far, vmem, vmem, vmem, vmem, far, far, far, far, far, vmem, vmem, vmem, vmem, vmem],
-        out_specs=(vmem, vmem, vmem, vmem),
+        out_specs=(vmem, vmem, far, far),
         scratch_shapes=[
             pltpu.VMEM(grid.shape, BF16),
             pltpu.VMEM(w_q_enc.shape, BF16),
@@ -397,7 +403,10 @@
             pltpu.VMEM((peers, nodes, width), BF16),
             pltpu.VMEM((peers, 2, HEADS * nodes), F32),
             pltpu.VMEM((peers, nodes, 2 * width), BF16),
+            pltpu.VMEM((points, width), BF16),
+            pltpu.VMEM((peers * nodes, points), F32),
             pltpu.SemaphoreType.DMA((6,)),
+            pltpu.SemaphoreType.DMA((2,)),
             pltpu.SemaphoreType.DMA((8, peers)),
             pltpu.SemaphoreType.DMA((8, peers)),
         ],
@@ -408,22 +417,25 @@
       w_kv_dec, enc_need, enc_slot.T, enc_count[None], dec_slot, dec_need.reshape(-1, 128))
 
 
-def decoder_kernel(query_ref, pairs_ref, bias_ref, grid_ref, wo_ref, latent_ref, out_ref, latent_out, keys_of, turned, mixed):
+def decoder_kernel(query_ref, pairs_ref, bias_ref, grid_hbm, wo_hbm, latent_ref, out_hbm, latent_out, keys_of, turned, mixed,
+                   grid_v, wo_v, out_v, load_sem, store_sem):
     tile, width = query_ref.shape
     head = width // HEADS
     keys = pairs_ref.shape[0]
     quad = 4
-
-    @pl.when(pl.program_id(0) == 0)
-    def _():
-        turned[...] = pairs_ref[:, width:].astype(F32).T.astype(BF16)
-        latent_out[...] = latent_ref[...]
-        lane_head = iota((keys, quad * head), 1) // head
-        for h in range(HEADS):
-            some = pairs_ref[:, (h // quad) * quad * head : (h // quad + 1) * quad * head] * (1.0 / math.sqrt(head))
-            keys_of[h // quad, (h % quad) * keys : (h % quad + 1) * keys, :] = jnp.where(
-                lane_head == h % quad, some, jnp.zeros_like(some)
-            )
+    load_wo = pltpu.make_async_copy(wo_hbm, wo_v, load_sem.at[0])
+    load_grid = pltpu.make_async_copy(grid_hbm, grid_v, load_sem.at[1])
+    load_wo.start()
+    load_grid.start()
+
+    turned[...] = pairs_ref[:, width:].astype(F32).T.astype(BF16)
+    latent_out[...] = latent_ref[...]
+    lane_head = iota((keys, quad * head), 1) // head
+    for h in range(HEADS):
+        some = pairs_ref[:, (h // quad) * quad * head : (h // quad + 1) * quad * head] * (1.0 / math.sqrt(head))
+        keys_of[h // quad, (h % quad) * keys : (h % quad + 1) * keys, :] = jnp.where(
+            lane_head == h % quad, some, jnp.zeros_like(some)
+        )
 
     for four in range(HEADS // quad):
         query = query_ref[:, four * quad * head : (four + 1) * quad * head]
@@ -436,33 +448,38 @@
             total = jnp.sum(raised, axis=0, keepdims=True)
             got = jnp.dot(turned[h * head : (h + 1) * head, :], raised.astype(BF16), preferred_element_type=F32)
             mixed[h * head : (h + 1) * head, :] = (got / total).astype(BF16)
-    update = lax.dot_general(mixed[...], wo_ref[...], TN, preferred_element_type=F32)
-    out_ref[...] = (grid_ref[...].astype(F32) + update).astype(BF16)
+    load_wo.wait()
+    load_grid.wait()
+    stores = []
+    block = tile // 4
+    for part in range(4):
+        at = slice(part * block, (part + 1) * block)
+        update = lax.dot_general(mixed[:, at], wo_v[...], TN, preferred_element_type=F32)
+        out_v[at, :] = (grid_v[at, :].astype(F32) + update).astype(BF16)
+        stores.append(pltpu.make_async_copy(out_v.at[at], out_hbm.at[at], store_sem.at[part]))
+        stores[-1].start()
+    for store in stores:
+        store.wait()
 
 
 def decode(queries, pairs, bias, grid, w_o_dec, latent_out):
     points, model = grid.shape
     width = queries.shape[1]
-    tile = 1024
-    whole = lambda shape: pl.BlockSpec(shape, lambda i: (0, 0))
+    tile = points
+    vmem = pl.BlockSpec(memory_space=pltpu.VMEM)
+    far = pl.BlockSpec(memory_space=pl.ANY)
     return pl.pallas_call(
         decoder_kernel,
         name="decode",
-        grid=(points // tile,),
         out_shape=(
             jax.ShapeDtypeStruct(grid.shape, BF16),
             jax.ShapeDtypeStruct(latent_out.shape, BF16),
         ),
-        in_specs=[
-            pl.BlockSpec((tile, width), lambda i: (i, 0)),
-            whole(pairs.shape),
-            pl.BlockSpec((pairs.shape[0], tile), lambda i: (0, i)),
-            pl.BlockSpec((tile, model), lambda i: (i, 0)),
-            whole(w_o_dec.shape),
-            whole(latent_out.shape),
-        ],
-        out_specs=(pl.BlockSpec((tile, model), lambda i: (i, 0)), whole(latent_out.shape)),
-        scratch_shapes=[pltpu.VMEM((2, 4 * pairs.shape[0], width // 2), BF16), pltpu.VMEM((width, pairs.shape[0]), BF16), pltpu.VMEM((width, tile), BF16)],
+        in_specs=[vmem, vmem, vmem, far, far, vmem],
+        out_specs=(far, vmem),
+        scratch_shapes=[pltpu.VMEM((2, 4 * pairs.shape[0], width // 2), BF16), pltpu.VMEM((width, pairs.shape[0]), BF16), pltpu.VMEM((width, tile), BF16),
+                        pltpu.VMEM(grid.shape, BF16), pltpu.VMEM(w_o_dec.shape, BF16), pltpu.VMEM(grid.shape, BF16),
+                        pltpu.SemaphoreType.DMA((2,)), pltpu.SemaphoreType.DMA((4,))],
     )(queries, pairs, bias, grid, w_o_dec, latent_out)
 
 
@@ -480,7 +497,7 @@
     peers = lax.axis_size("dom")
     cap = enc_need.shape[1] // peers
     small = latent_in.shape[0] * peers <= 256
-    fits = peers % 2 == 0 and 128 % cap == 0 and cap % 32 == 0 and HEADS * latent_in.shape[0] == 128 and grid.shape[0] % 1024 == 0
+    fits = peers % 2 == 0 and 128 % cap == 0 and cap % 32 == 0 and HEADS * latent_in.shape[0] == 128 and grid.shape[0] % 512 == 0
     if small and fits and 8 % dec_slot.shape[0] == 0:
         return by_kernels(*args)
     return on_device(*args)

time: 45.8 us -> 43.9 us (0.959)
  Pallas kernels: 44.7 us -> 43 us
    pallas_call x1, Pallas kernels: 35.1 us -> 34.1 us  [encode(): pl.pallas_call(functools.partial(encoder_kernel, peers), name='encode', o...]
    pallas_call x1, Pallas kernels: 9.55 us -> 8.86 us  [decode(): pl.pallas_call(decoder_kernel, name='decode', out_shape=(jax.ShapeDtypeSt...]
where the time goes in v5:
time: 43.9 us; the launch traced here: 43.6 us
  Pallas kernels  43 us (98%)
  between operations  0.64 us (1%)
    pallas_call x1, Pallas kernels, encode(): pl.pallas_call(functools.partial(encoder_kernel, peers), name='encode', o...  34.1 us
    pallas_call x1, Pallas kernels, decode(): pl.pallas_call(decoder_kernel, name='decode', out_shape=(jax.ShapeDtypeSt...  8.86 us

profile of v5, /device:TPU:0, one launch (start us, length us, event | category | flops | bytes accessed | tf_op | source)
XLA Modules:
  0.0 43.6 jit_solution(18145427265022984165)
XLA Ops:
  0.6 34.1 %encode.1 = (bf16[16,1024]{1,0:T(8,128)(2,1)}, bf16[256,1024]{1,0:T(8,128)(2,1)}, bf16[1024,512]{1,0:T(8,128)(2,1)}, f32[256,1024]{1,0:T(8,128)}) custom-call(bf16[1024,1024]{1,0:T(8,128)(2,1)} %grid_hbm.3, bf16[16,1024]{1,0:T(8,128)(2,1)} %latent_ref.1, f32[1,1024]{1,0:T(1,128)} %bitcast.8, f32[1,1024]{1,0:T(1,128)} %bitcast.9, f32[1,1024]{1,0:T(1,128)} %bitcast.10, ...), custom_call_target="tpu_custom_call" | custom-call | tf_op jit(solution)/shard_map/encode/pallas_call | solution.py:375
  34.8 8.9 %decode.1 = (bf16[1024,1024]{1,0:T(8,128)(2,1)}, bf16[16,1024]{1,0:T(8,128)(2,1)}) custom-call(bf16[1024,512]{1,0:T(8,128)(2,1)} %get-tuple-element.8.query_ref, bf16[256,1024]{1,0:T(8,128)(2,1)} %get-tuple-element.9.pairs_ref, f32[256,1024]{1,0:T(8,128)} %get-tuple-element.10.bias_ref, bf16[1024,1024]{1,0:T(8,128)(2,1)} %grid_hbm.3, ...), custom_call_target="tpu_custom_call" | custom-call | tf_op jit(solution)/shard_map/decode/pallas_call | solution.py:471
